TPU v7x, 32 devices: a whole 2x2x4 slice. The times are simulated.
32 devices in a mesh: ctx: 4 (over y, x), exp: 8 (over z, core).
Axes of the slice: x: 2, y: 2, z: 4, core: 2. Of those that a mesh axis runs over, the one named last changes fastest.
Arguments:
- queries: bfloat16 [512, 12288], P('ctx', 'exp'), may hold values from -40.35234 to 40.35234
- key_rows: bfloat16 [512, 12288], P('ctx', 'exp'), may hold values from -4 to 4
- value_rows: bfloat16 [512, 8192], P('ctx', 'exp'), may hold values from -6 to 6
- w_out: bfloat16 [8192, 3584], P('exp'), may hold values from -0.5 to 0.5
- residual: bfloat16 [512, 3584], P(('ctx', 'exp')), may hold values from -3 to 3
- norm_gain: float32 [3584], replicated, may hold values from 0.1 to 1.9
- router: bfloat16 [3584, 32], replicated, may hold values from -0.09375 to 0.09375
- routing: int32 [8, 4, 16, 8], P('exp'), may hold values from 0 to 31, all different within a row; in each aligned block of 64 rows (0 to 63, 64 to 127, ..., all dimensions but the last counted through in order) at most 24 rows name the same one
- w_gate: bfloat16 [32, 3584, 2048], P('exp', None, 'ctx'), may hold values from -0.09375 to 0.09375
- w_up: bfloat16 [32, 3584, 2048], P('exp', None, 'ctx'), may hold values from -0.09375 to 0.09375
- w_down: bfloat16 [32, 2048, 3584], P('exp', 'ctx'), may hold values from -0.125 to 0.125
Outputs:
- mixed: bfloat16 [512, 3584], P(('ctx', 'exp'))
Inputs may be any that keep to these rules, and one draw needn't show every extreme that they name: `routing`: each token lists 8 different experts. Among the 64 tokens at one index of the first dimension, no expert is listed more than 24 times, and in every draw some expert is listed exactly 24 times in some such group.
All inputs are finite; a program needn't handle non-finite values.
Results may differ from a plain program's by a relative error of at most 0.025.
Values may be sent and summed in bfloat16 or wider, within the bound.
A program may use at most 128 MiB of HBM per device.

v0:
```python
import jax
import jax.numpy as jnp
from jax import lax
from jax.sharding import PartitionSpec as P

DQK = 192
DV = 128


NEG = -1e30


def from_behind(block, axis, distance):
    devices = range(lax.axis_size(axis))
    route = [((i - distance) % len(devices), i) for i in devices]
    return lax.ppermute(block, axis, route)


def body(
    queries, key_rows, value_rows, w_out, residual, norm_gain, router, routing, w_gate, w_up, w_down
):
    ctx_index = lax.axis_index("ctx")
    ctx_count = lax.axis_size("ctx")
    tok_rows = queries.shape[0]
    heads_here = queries.shape[1] // DQK
    q_full = queries.reshape(tok_rows, heads_here, DQK)
    k_full = key_rows.reshape(tok_rows, heads_here, DQK)
    v_full = value_rows.reshape(tok_rows, heads_here, DV)
    positions = jnp.arange(tok_rows, dtype=jnp.int32)
    score_scale = DQK ** (-0.5)

    def attend(state, q_part, k_part, v_part, q_source, k_source):
        row_max, row_total, accum = state
        scores = (
            jnp.einsum("thd,shd->hts", q_part, k_part, preferred_element_type=jnp.float32)
            * score_scale
        )
        query_pos = q_source * tok_rows + positions
        key_pos = k_source * tok_rows + positions
        allowed = (key_pos[None, :] <= query_pos[:, None])[None]
        scores = jnp.where(allowed, scores, NEG)
        new_max = jnp.maximum(row_max, jnp.max(scores, axis=-1))
        probs = jnp.where(allowed, jnp.exp(scores - new_max[..., None]), 0.0)
        carry_scale = jnp.exp(row_max - new_max)
        row_total = row_total * carry_scale + jnp.sum(probs, axis=-1)
        accum = accum * carry_scale[..., None] + jnp.einsum(
            "hts,shd->htd", probs, v_part.astype(jnp.float32), precision=lax.Precision.HIGHEST
        )
        return (new_max, row_total, accum)

    def visit(state, q_part, k_part, v_part, q_source, k_source):
        return attend(state, q_part, k_part, v_part, q_source, k_source)

    home = visit(
        (
            jnp.full((heads_here, tok_rows), NEG, jnp.float32),
            jnp.zeros((heads_here, tok_rows), jnp.float32),
            jnp.zeros((heads_here, tok_rows, DV), jnp.float32),
        ),
        q_full,
        k_full,
        v_full,
        ctx_index,
        ctx_index,
    )

    def turn(turn_index, carry):
        state, k_now, v_now = carry
        k_now, v_now = from_behind((k_now, v_now), "ctx", -1)
        source = (ctx_index + turn_index + 1) % ctx_count
        state = visit(state, q_full, k_now, v_now, ctx_index, source)
        return (state, k_now, v_now)

    carried = lax.fori_loop(0, ctx_count - 1, turn, (home, k_full, v_full))
    row_total, accum = (carried[0][1], carried[0][2])
    final = accum / row_total[..., None]
    attended = final.transpose(1, 0, 2).reshape(tok_rows, heads_here * DV).astype(jnp.bfloat16)
    attn_out = lax.psum_scatter(
        jnp.dot(attended, w_out, preferred_element_type=jnp.float32).astype(jnp.bfloat16),
        "exp",
        scatter_dimension=0,
        tiled=True,
    ).astype(jnp.float32)
    hidden_state = residual.astype(jnp.float32) + attn_out
    mean_square = jnp.mean(hidden_state * hidden_state, axis=-1, keepdims=True)
    normed = (hidden_state * lax.rsqrt(mean_square + 1e-06) * norm_gain).astype(jnp.bfloat16)
    column = lax.all_gather(normed, "ctx", axis=0, tiled=True)
    experts = router.shape[1]
    top_count = routing.shape[-1]
    routes = routing.reshape(-1, top_count)
    group_rows = routes.shape[0]
    capacity = 3 * group_rows * top_count // (2 * experts)
    d_model = column.shape[1]
    affinity = jax.nn.sigmoid(jnp.dot(column, router, preferred_element_type=jnp.float32))
    onehot = routes[:, :, None] == jnp.arange(experts, dtype=jnp.int32)[None, None, :]
    chosen = jnp.sum(jnp.where(onehot, affinity[:, None, :], 0.0), axis=-1)
    route_weight = 2.5 * chosen / jnp.sum(chosen, axis=-1, keepdims=True)
    flat_hot = onehot.reshape(group_rows * top_count, experts).astype(jnp.int32)
    before = jnp.cumsum(flat_hot, axis=0) - flat_hot
    slot_index = jnp.sum(before * flat_hot, axis=-1)
    target = routes.reshape(-1) * capacity + slot_index
    matches = (target[:, None] == jnp.arange(experts * capacity, dtype=jnp.int32)[None, :]).reshape(
        group_rows, top_count, experts * capacity
    )
    dispatch_table = jnp.any(matches, axis=1).T.astype(jnp.bfloat16)
    outgoing = jnp.dot(dispatch_table, column, preferred_element_type=jnp.float32).astype(
        jnp.bfloat16
    )
    outgoing = outgoing.reshape(experts, capacity, d_model)
    arrived = lax.all_to_all(outgoing, "exp", split_axis=0, concat_axis=0, tiled=True)
    local_experts = w_gate.shape[0]
    sources = arrived.shape[0] // local_experts
    slots_here = arrived.shape[1]
    inputs = arrived.reshape(sources, local_experts, slots_here, d_model)
    gate = jnp.einsum("sexd,edf->sexf", inputs, w_gate, preferred_element_type=jnp.float32)
    upper = jnp.einsum("sexd,edf->sexf", inputs, w_up, preferred_element_type=jnp.float32)
    expert_hidden = (jax.nn.silu(gate) * upper).astype(jnp.bfloat16)
    partial_value = jnp.einsum(
        "sexf,efd->sexd", expert_hidden, w_down, preferred_element_type=jnp.float32
    ).astype(jnp.bfloat16)
    partial_value = partial_value.reshape(sources * local_experts, slots_here, d_model)
    returned = lax.all_to_all(partial_value, "exp", split_axis=0, concat_axis=0, tiled=True)
    flat_back = returned.reshape(experts * capacity, d_model)
    picked = (
        jnp.take(flat_back, target, axis=0)
        .reshape(group_rows, top_count, d_model)
        .astype(jnp.float32)
    )
    combined = jnp.sum(picked * route_weight[..., None], axis=1)
    moe_out = lax.psum_scatter(
        combined.astype(jnp.bfloat16), "ctx", scatter_dimension=0, tiled=True
    ).astype(jnp.float32)
    return (hidden_state + moe_out).astype(jnp.bfloat16)


def solution(mesh):
    in_specs = (
        P("ctx", "exp"),
        P("ctx", "exp"),
        P("ctx", "exp"),
        P("exp", None),
        P(("ctx", "exp"), None),
        P(),
        P(),
        P("exp", None, None, None),
        P("exp", None, "ctx"),
        P("exp", None, "ctx"),
        P("exp", "ctx", None),
    )
    out_specs = P(("ctx", "exp"), None)
    return jax.shard_map(body, mesh=mesh, in_specs=in_specs, out_specs=out_specs, check_vma=False)
```

profile of v0, /device:TPU:0, one launch (start us, length us, event | category | flops | bytes accessed | tf_op | source)
XLA Modules:
  0.0 447.0 jit_solution(17789973888606974906)
XLA Ops:
  6.6 1.1 copy.40
  7.8 0.2 copy.43
  8.0 1.2 copy.38
  9.2 1.2 copy.39
  10.4 0.4 fusion.46
  10.8 0.1 fusion.35
  10.9 0.6 convolution_add_fusion.1
  11.6 54.3 %while.25 = (s32[]{:T(128)}, f32[8,128]{1,0:T(8,128)S(1)}, f32[8,128]{1,0:T(8,128)S(1)}, f32[8,128,128]{2,1,0:T(8,128)S(1)}, bf16[128,8,192]{0,2,1:T(8,128)(2,1)...) while((s32[]{:T(128)}, f32[8,128]{1,0:T(8,128)S(1)}, ...), condition=%wide.region_5.6_spmd.clone.clone, body=%wide.region_2.5_spmd.clone.clone.sunk | while | flops 252987664 | bytes 7735662 | solution.py:74
  11.6 4.0 collective-permute-start
  15.6 0.5 collective-permute-start.1
  16.2 13.4 %collective-permute-done.1 = bf16[128,8,128]{2,0,1:T(8,128)(2,1)S(1)} collective-permute-done((bf16[128,8,128]{2,0,1:T(8,128)(2,1)S(1)}, bf16[128,8,128]{2,0,1:T(8,128)(2,1)S(1)}, u32[]{:S(2)}, u32[]{:S(2)}) %collective-permute-start.1) | collective-permute-done | bytes 262176 | tf_op jit(solution)/shard_map/while/body/eval_jaxpr/ppermute | solution.py:16
  29.6 0.4 fusion.68
  30.0 0.1 fusion.69
  30.1 0.8 convolution_add_fusion.3
  30.9 3.4 collective-permute-start
  34.5 13.0 %collective-permute-done.1 = bf16[128,8,128]{2,0,1:T(8,128)(2,1)S(1)} collective-permute-done((bf16[128,8,128]{2,0,1:T(8,128)(2,1)S(1)}, bf16[128,8,128]{2,0,1:T(8,128)(2,1)S(1)}, u32[]{:S(2)}, u32[]{:S(2)}) %collective-permute-start.1) | collective-permute-done | bytes 262176 | tf_op jit(solution)/shard_map/while/body/eval_jaxpr/ppermute | solution.py:16
  47.5 0.4 fusion.68
  47.9 0.1 fusion.69
  48.1 0.8 convolution_add_fusion.3
  48.8 3.4 collective-permute-start
  52.4 12.1 %collective-permute-done.1 = bf16[128,8,128]{2,0,1:T(8,128)(2,1)S(1)} collective-permute-done((bf16[128,8,128]{2,0,1:T(8,128)(2,1)S(1)}, bf16[128,8,128]{2,0,1:T(8,128)(2,1)S(1)}, u32[]{:S(2)}, u32[]{:S(2)}) %collective-permute-start.1) | collective-permute-done | bytes 262176 | tf_op jit(solution)/shard_map/while/body/eval_jaxpr/ppermute | solution.py:16
  64.6 0.4 fusion.68
  65.0 0.1 fusion.69
  65.1 0.8 convolution_add_fusion.3
  65.9 0.2 copy.44
  66.2 5.2 %convolution_convert_fusion.1 = bf16[128,3584]{1,0:T(8,128)(2,1)} fusion(bf16[128,1024]{0,1:T(8,128)(2,1)S(1)} %bitcast.110, bf16[1024,3584]{1,0:T(8,128)(2,1)} %param.16), kind=kOutput, calls=%fused_computation.28 | convolution fusion | flops 939982848 | bytes 8519680 | tf_op jit(solution)/shard_map/dot_general | solution.py:79
  71.8 1.2 reduce-window.6
  73.0 0.2 slice_reduce_fusion
  73.2 0.1 fusion.41
  73.6 0.5 fusion.26
  74.2 31.8 %reduce-scatter.3.cloned.1.call-done = bf16[16,3584]{1,0:T(8,128)(2,1)} async-done(((bf16[128,3584]{1,0:T(8,128)(2,1)}), bf16[16,3584]{1,0:T(8,128)(2,1)}) %reduce-scatter.3.cloned.1.call-update) | async-done | bytes 114704 | tf_op jit(solution)/shard_map/reduce_scatter | solution.py:78
  106.0 1.0 multiply_reduce_fusion.1
  107.0 1.0 multiply_convert_fusion
  108.0 9.8 %all_gather.3 = bf16[64,3584]{1,0:T(8,128)(2,1)S(1)} all-gather(bf16[16,3584]{1,0:T(8,128)(2,1)S(1)} %multiply_convert_fusion), channel_id=1, replica_groups=mesh['ctx'=4,'exp'=8] {'ctx'}, dimensions={0}, use_global_device_ids=true | all-gather | bytes 573440 | tf_op jit(solution)/shard_map/all_gather | solution.py:87
  117.8 1.6 convolution_convert_fusion
  119.4 124.6 %all_to_all.10 = bf16[32,24,3584]{2,1,0:T(8,128)(2,1)S(1)} all-to-all(bf16[32,24,3584]{2,1,0:T(8,128)(2,1)S(1)} %bitcast.102), channel_id=1, replica_groups=mesh['ctx'=4,'exp'=8] {'exp'}, dimensions={0} | all-to-all | bytes 11010048 | tf_op jit(solution)/shard_map/all_to_all | solution.py:110
  244.0 6.9 %fusion.12 = f32[4,8,24,512]{3,2,1,0:T(8,128)S(1)} fusion(bf16[4,3584,512]{2,1,0:T(8,128)(2,1)} %param.21, bf16[8,4,24,3584]{3,2,1,0:T(8,128)(2,1)S(1)} %bitcast.106), kind=kOutput, calls=%fused_computation.20 | convolution fusion | flops 2818572288 | bytes 21757952 | tf_op jit(solution)/shard_map/sexd,edf->sexf/dot_general | solution.py:115
  250.9 8.6 %fusion.22 = bf16[8,4,24,512]{3,2,0,1:T(8,128)(2,1)S(1)} fusion(f32[4,8,24,512]{3,2,1,0:T(8,128)S(1)} %fusion.12, bf16[4,3584,512]{2,1,0:T(8,128)(2,1)} %param.22, bf16[8,4,24,3584]{3,2,1,0:T(8,128)(2,1)S(1)} %bitcast.107), kind=kOutput, calls=%fused_computation.31 | convolution fusion | flops 2820931584 | bytes 22544384 | tf_op jit(solution)/shard_map/sexd,edf->sexf/dot_general | solution.py:116
  259.5 8.2 %fusion.17 = bf16[8,4,24,3584]{3,2,0,1:T(8,128)(2,1)S(1)} fusion(bf16[8,4,24,512]{3,2,0,1:T(8,128)(2,1)S(1)} %fusion.22, bf16[4,512,3584]{2,1,0:T(8,128)(2,1)} %param.23), kind=kOutput, calls=%fused_computation.25 | convolution fusion | flops 2821324800 | bytes 20971520 | tf_op jit(solution)/shard_map/sexf,efd->sexd/dot_general | solution.py:118
  267.7 3.0 copy.54
  270.7 4.7 %all-to-all-start.1 = ((bf16[32,24,3584]{2,1,0:T(8,128)(2,1)}), bf16[32,24,3584]{2,1,0:T(8,128)(2,1)}, u32[]{:S(2)}, u32[]{:S(2)}) async-start(bf16[32,24,3584]{2,1,0:T(8,128)(2,1)} %bitcast.103), calls=%async_computation.2 | async-start | bytes 11010048 | tf_op jit(solution)/shard_map/all_to_all | solution.py:122
  275.4 0.3 reduce-scatter.5.cloned.1.call-start
  276.0 0.3 fusion.34
  276.4 121.1 %all-to-all-done.1 = bf16[32,24,3584]{2,1,0:T(8,128)(2,1)} async-done(((bf16[32,24,3584]{2,1,0:T(8,128)(2,1)}), bf16[32,24,3584]{2,1,0:T(8,128)(2,1)}, u32[]{:S(2)}, u32[]{:S(2)}) %all-to-all-start.1) | async-done | bytes 5505056 | tf_op jit(solution)/shard_map/all_to_all | solution.py:122
  397.5 11.3 %gather_fusion = bf16[512,3584]{1,0:T(8,128)(2,1)} fusion(bf16[768,3584]{1,0:T(8,128)(2,1)} %bitcast.18, s32[1024]{0:T(1024)S(1)} %pad_clamp_fusion), kind=kCustom, calls=%fused_computation | custom fusion | bytes 7342080 | tf_op jit(solution)/shard_map/jit(_take)/gather | solution.py:125
  408.8 6.8 %multiply_reduce_fusion = bf16[64,3584]{1,0:T(8,128)(2,1)} fusion(bf16[512,3584]{1,0:T(8,128)(2,1)} %gather_fusion, f32[64,8]{1,0:T(8,128)S(1)} %copy.56, pred[64,8]{1,0:T(8,128)(4,1)S(1)} %copy.50), kind=kLoop, calls=%fused_computation.22 | loop fusion | flops 7110656 | bytes 4131328 | tf_op jit(solution)/shard_map/reduce_sum | solution.py:129
  415.6 23.0 %reduce-scatter.5.cloned.1.call-done = bf16[16,3584]{1,0:T(8,128)(2,1)} async-done(((bf16[64,3584]{1,0:T(8,128)(2,1)}), bf16[16,3584]{1,0:T(8,128)(2,1)}) %reduce-scatter.5.cloned.1.call-update) | async-done | bytes 114704 | tf_op jit(solution)/shard_map/reduce_scatter | solution.py:130
  438.5 1.6 add_convert_fusion
  (66 shorter events, 1.9 us)
Async XLA Ops:
  6.5 269.5 %copy-start = (bf16[3584,32]{0,1:T(8,128)(2,1)S(1)}, bf16[3584,32]{0,1:T(8,128)(2,1)}, u32[]{:S(2)}) copy-start(bf16[3584,32]{0,1:T(8,128)(2,1)} %param.19) | copy-start | bytes 688132
  6.5 99.4 %reduce-scatter.3.cloned.1.call-start = ((), (), s32[]{:S(2)}) async-start(), calls=%async_computation.4 | async-start | bytes 1032192 | tf_op jit(solution)/shard_map/reduce_scatter | solution.py:78
  11.6 18.0 %collective-permute-start = (bf16[128,8,192]{0,2,1:T(8,128)(2,1)S(1)}, bf16[128,8,192]{0,2,1:T(8,128)(2,1)S(1)}, u32[]{:S(2)}, u32[]{:S(2)}) collective-permute-start(bf16[128,8,192]{0,2,1:T(8,128)(2,1)S(1)} %get-tuple-element.417), channel_id=1, source_target_pairs={{8,0},{16,8},{24,16},{0,24},{9,1},{17,9},{25,17},{1,25},{10,2},{18... | collective-permute-start | bytes 1179656 | tf_op jit(solution)/shard_map/while/body/eval_jaxpr/ppermute | solution.py:16
  15.6 14.0 %collective-permute-start.1 = (bf16[128,8,128]{2,0,1:T(8,128)(2,1)S(1)}, bf16[128,8,128]{2,0,1:T(8,128)(2,1)S(1)}, u32[]{:S(2)}, u32[]{:S(2)}) collective-permute-start(bf16[128,8,128]{2,0,1:T(8,128)(2,1)S(1)} %get-tuple-element.418), channel_id=1, source_target_pairs={{8,0},{16,8},{24,16},{0,24},{9,1},{17,9},{25,17},{1,25},{10,2},{18... | collective-permute-start | bytes 786440 | tf_op jit(solution)/shard_map/while/body/eval_jaxpr/ppermute | solution.py:16
  30.9 16.6 %collective-permute-start = (bf16[128,8,192]{0,2,1:T(8,128)(2,1)S(1)}, bf16[128,8,192]{0,2,1:T(8,128)(2,1)S(1)}, u32[]{:S(2)}, u32[]{:S(2)}) collective-permute-start(bf16[128,8,192]{0,2,1:T(8,128)(2,1)S(1)} %get-tuple-element.417), channel_id=1, source_target_pairs={{8,0},{16,8},{24,16},{0,24},{9,1},{17,9},{25,17},{1,25},{10,2},{18... | collective-permute-start | bytes 1179656 | tf_op jit(solution)/shard_map/while/body/eval_jaxpr/ppermute | solution.py:16
  34.4 13.1 %collective-permute-start.1 = (bf16[128,8,128]{2,0,1:T(8,128)(2,1)S(1)}, bf16[128,8,128]{2,0,1:T(8,128)(2,1)S(1)}, u32[]{:S(2)}, u32[]{:S(2)}) collective-permute-start(bf16[128,8,128]{2,0,1:T(8,128)(2,1)S(1)} %get-tuple-element.418), channel_id=1, source_target_pairs={{8,0},{16,8},{24,16},{0,24},{9,1},{17,9},{25,17},{1,25},{10,2},{18... | collective-permute-start | bytes 786440 | tf_op jit(solution)/shard_map/while/body/eval_jaxpr/ppermute | solution.py:16
  48.8 15.7 %collective-permute-start = (bf16[128,8,192]{0,2,1:T(8,128)(2,1)S(1)}, bf16[128,8,192]{0,2,1:T(8,128)(2,1)S(1)}, u32[]{:S(2)}, u32[]{:S(2)}) collective-permute-start(bf16[128,8,192]{0,2,1:T(8,128)(2,1)S(1)} %get-tuple-element.417), channel_id=1, source_target_pairs={{8,0},{16,8},{24,16},{0,24},{9,1},{17,9},{25,17},{1,25},{10,2},{18... | collective-permute-start | bytes 1179656 | tf_op jit(solution)/shard_map/while/body/eval_jaxpr/ppermute | solution.py:16
  52.3 12.3 %collective-permute-start.1 = (bf16[128,8,128]{2,0,1:T(8,128)(2,1)S(1)}, bf16[128,8,128]{2,0,1:T(8,128)(2,1)S(1)}, u32[]{:S(2)}, u32[]{:S(2)}) collective-permute-start(bf16[128,8,128]{2,0,1:T(8,128)(2,1)S(1)} %get-tuple-element.418), channel_id=1, source_target_pairs={{8,0},{16,8},{24,16},{0,24},{9,1},{17,9},{25,17},{1,25},{10,2},{18... | collective-permute-start | bytes 786440 | tf_op jit(solution)/shard_map/while/body/eval_jaxpr/ppermute | solution.py:16
  66.2 5.3 %copy-start.3 = (s32[1,4,16,8]{2,3,1,0:T(8,128)S(1)}, s32[1,4,16,8]{2,3,1,0:T(8,128)}, u32[]{:S(2)}) copy-start(s32[1,4,16,8]{2,3,1,0:T(8,128)} %param.20) | copy-start | bytes 6148
  66.2 39.8 %copy-start.1 = (bf16[16,3584]{1,0:T(8,128)(2,1)S(1)}, bf16[16,3584]{1,0:T(8,128)(2,1)}, u32[]{:S(2)}) copy-start(bf16[16,3584]{1,0:T(8,128)(2,1)} %param.17) | copy-start | bytes 344068
  66.2 40.8 %copy-start.4 = (f32[3584]{0:T(1024)S(1)}, f32[3584]{0:T(1024)}, u32[]{:S(2)}) copy-start(f32[3584]{0:T(1024)} %param.18) | copy-start | bytes 43012
  270.7 126.7 %all-to-all-start.1 = ((bf16[32,24,3584]{2,1,0:T(8,128)(2,1)}), bf16[32,24,3584]{2,1,0:T(8,128)(2,1)}, u32[]{:S(2)}, u32[]{:S(2)}) async-start(bf16[32,24,3584]{2,1,0:T(8,128)(2,1)} %bitcast.103), calls=%async_computation.2 | async-start | bytes 11010048 | tf_op jit(solution)/shard_map/all_to_all | solution.py:122
  275.4 163.1 %reduce-scatter.5.cloned.1.call-start = ((), (), s32[]{:S(2)}) async-start(), calls=%async_computation.5 | async-start | bytes 573440 | tf_op jit(solution)/shard_map/reduce_scatter | solution.py:130
  397.5 41.1 %copy-start.2 = (bf16[16,3584]{1,0:T(8,128)(2,1)S(1)}, bf16[16,3584]{1,0:T(8,128)(2,1)}, u32[]{:S(2)}) copy-start(bf16[16,3584]{1,0:T(8,128)(2,1)} %reduce-scatter.3.cloned.1.call-done) | copy-start | bytes 344068
Sparse Core Ops, SparseCore 0:
  71.6 34.3 reduce-scatter.2
  415.7 22.7 reduce-scatter.4
where the time goes:
time: 447 us
  waiting for transfers between devices  214 us (48%)
  blocking collectives  134 us (30%)
  matrix products  35.1 us (8%)
  local copies, waits for them, and re-layouts  19.6 us (4%)
  starting transfers between devices  16.4 us (4%)
  between operations  13.7 us (3%)
  other arithmetic  13.3 us (3%)
    all_to_all x1, blocking collectives, body(): lax.all_to_all(outgoing, 'exp', split_axis=0, concat_axis=0, tiled=True)  125 us
    all_to_all x1, waiting for transfers between devices, body(): lax.all_to_all(partial_value, 'exp', split_axis=0, concat_axis=0, tiled=T...  121 us
    ppermute x6, waiting for transfers between devices, from_behind(): return lax.ppermute(block, axis, route)  38.4 us
    reduce_scatter x1, waiting for transfers between devices, body(): lax.psum_scatter(jnp.dot(attended, w_out, preferred_element_type=jnp.floa...  31.8 us
    reduce_scatter x1, waiting for transfers between devices, body(): lax.psum_scatter(combined.astype(jnp.bfloat16), 'ctx', scatter_dimension=...  23 us
    ppermute x6, starting transfers between devices, from_behind(): return lax.ppermute(block, axis, route)  11.5 us
    gather x1, local copies, waits for them, and re-layouts, body(): jnp.take(flat_back, target, axis=0).reshape(group_rows, top_count, d_model)  11.3 us
    all_gather x1, blocking collectives, body(): column = lax.all_gather(normed, 'ctx', axis=0, tiled=True)  9.75 us
  transfers between devices with their start and end apart: 9, of which 6 were waited for; matrix products, arithmetic and copies ran while one was open for 1% of the time, Pallas kernels for 0%

commit v1 on v0

--- a/solution.py
+++ b/solution.py
@@ -1,6 +1,10 @@
+import functools
+
 import jax
 import jax.numpy as jnp
 from jax import lax
+from jax.experimental import pallas as pl
+from jax.experimental.pallas import tpu as pltpu
 from jax.sharding import PartitionSpec as P
 
 DQK = 192
@@ -8,6 +12,363 @@
 
 
 NEG = -1e30
+MESH = pl.DeviceIdType.MESH
+
+
+def parts_of(width):
+    for count in (7, 4, 2, 3, 5):
+        if width % (count * 128) == 0:
+            return count
+    return 1
+
+
+def greet(nc, ne, c, e):
+    barrier = pltpu.get_barrier_semaphore()
+    for dc in range(1, nc):
+        pl.semaphore_signal(
+            barrier, inc=1, device_id=(lax.rem(c + dc, nc), e), device_id_type=MESH
+        )
+    for de in range(1, ne):
+        pl.semaphore_signal(
+            barrier, inc=1, device_id=(c, lax.rem(e + de, ne)), device_id_type=MESH
+        )
+    pl.semaphore_wait(barrier, nc + ne - 2)
+
+
+def remote(src, dst, send, recv, device):
+    return pltpu.make_async_remote_copy(
+        src_ref=src, dst_ref=dst, send_sem=send, recv_sem=recv, device_id=device, device_id_type=MESH
+    )
+
+
+def front_kernel(
+    nc, ne, heads,
+    q_ref, k_ref, v_ref, w_hbm, res_ref, gain_ref, route_ref,
+    hid_ref, full_ref, routes_ref,
+    qb, kb, vb, ab, att, wbuf, part, r1, sb, r2,
+    w_sem, a_send, a_recv, b_send, b_recv, e_send, e_recv,
+    s1_send, s1_recv, s2_send, s2_recv,
+    z_send, z_recv, c_send, c_recv, p_send, p_recv,
+):
+    c = lax.axis_index("ctx")
+    e = lax.axis_index("exp")
+    nz = ne // 2
+    z, core = e // 2, lax.rem(e, 2)
+    partner = (c, z * 2 + (1 - core))
+    tok = q_ref.shape[0]
+    wq, wv = heads * DQK, heads * DV
+    n_parts, width = part.shape[0], part.shape[-1]
+    d_model = hid_ref.shape[1]
+    w_copy = pltpu.make_async_copy(w_hbm, wbuf, w_sem)
+    w_copy.start()
+    greet(nc, ne, c, e)
+    sent = []
+
+    def launch(copy):
+        copy.start()
+        sent.append(copy)
+
+    triples = ((k_ref, kb, wq), (q_ref, qb, wq), (v_ref, vb, wv))
+    mine = pl.ds(pl.multiple_of(c * tok, tok), tok)
+    for dc in (list(range(1, nc))):
+        to = lax.rem(c + dc, nc)
+        for i, (src, buf, w) in enumerate(triples):
+            cols = pl.ds(pl.multiple_of(to * w, 128), w)
+            launch(remote(src.at[:, cols], buf.at[mine, :], a_send.at[i, dc], a_recv.at[i, dc], (to, e)))
+    for de in range(1, ne):
+        launch(
+            remote(route_ref, routes_ref.at[e], e_send.at[de], e_recv.at[de], (c, lax.rem(e + de, ne)))
+        )
+    routes_ref[e] = route_ref[...]
+    for src, buf, w in triples:
+        buf[mine, :] = src[:, pl.ds(pl.multiple_of(c * w, 128), w)]
+    for dc in range(1, nc):
+        origin = lax.rem(c + nc - dc, nc)
+        theirs = pl.ds(pl.multiple_of(origin * tok, tok), tok)
+        for i, (src, buf, w) in enumerate(triples):
+            remote(src.at[:, pl.ds(0, w)], buf.at[theirs, :], a_send.at[i, dc], a_recv.at[i, dc], (origin, e)).wait_recv()
+
+    own_cols = pl.ds(pl.multiple_of(c * wv, 128), wv)
+    for i in range(nc):
+        rows = pl.ds(i * tok, tok)
+        keys = (i + 1) * tok
+        q_i = qb[rows, :].astype(jnp.float32)
+        column = lax.broadcasted_iota(jnp.int32, (tok, wq), 1)
+        row_pos = i * tok + lax.broadcasted_iota(jnp.int32, (tok, keys), 0)
+        key_pos = lax.broadcasted_iota(jnp.int32, (tok, keys), 1)
+        allowed = key_pos <= row_pos
+        for h in range(heads):
+            inside = (column >= h * DQK) & (column < (h + 1) * DQK)
+            q_h = jnp.where(inside, q_i, 0.0).astype(jnp.bfloat16)
+            scores = lax.dot_general(
+                q_h, kb[0:keys, :], (((1,), (1,)), ((), ())), preferred_element_type=jnp.float32
+            ) * (DQK ** (-0.5))
+            scores = jnp.where(allowed, scores, NEG)
+            top = jnp.max(scores, axis=-1, keepdims=True)
+            probs = jnp.where(allowed, jnp.exp(scores - top), 0.0)
+            total = jnp.sum(probs, axis=-1, keepdims=True)
+            weighted = jnp.dot(
+                probs.astype(jnp.bfloat16),
+                vb[0:keys, h * DV : (h + 1) * DV],
+                preferred_element_type=jnp.float32,
+            )
+            ab[rows, h * DV : (h + 1) * DV] = (weighted / total).astype(jnp.bfloat16)
+
+        @pl.when(c != i)
+        def _():
+            remote(ab.at[rows, :], att.at[:, own_cols], b_send.at[i], b_recv.at[c], (i, e)).start()
+
+        @pl.when(c == i)
+        def _():
+            att[:, own_cols] = ab[rows, :]
+
+    w_copy.wait()
+    for j in range(nc):
+
+        @pl.when(c != j)
+        def _():
+            back = remote(ab.at[pl.ds(j * tok, tok), :], att.at[:, pl.ds(j * wv, wv)], b_send.at[j], b_recv.at[j], (j, e))
+            back.wait()
+
+    sub = tok // ne
+    for p in range(n_parts):
+        cols = slice(p * width, (p + 1) * width)
+        term = jnp.dot(att[...], wbuf[:, cols], preferred_element_type=jnp.float32)
+        part[p] = term.astype(jnp.bfloat16).reshape(nz, 2, sub, width)
+        launch(remote(part.at[p, :, 1 - core], r1.at[p], s1_send.at[p], s1_recv.at[p], partner))
+    for p in range(n_parts):
+        remote(part.at[p, :, 1 - core], r1.at[p], s1_send.at[p], s1_recv.at[p], partner).wait_recv()
+        sb[p] = (part[p, :, core].astype(jnp.float32) + r1[p].astype(jnp.float32)).astype(jnp.bfloat16)
+        for dz in range(1, nz):
+            zt = lax.rem(z + dz, nz)
+            launch(remote(sb.at[p, zt], r2.at[p, dz], s2_send.at[p, dz], s2_recv.at[p, dz], (c, zt * 2 + core)))
+    square = jnp.zeros((sub, 1), jnp.float32)
+    for p in range(n_parts):
+        cols = slice(p * width, (p + 1) * width)
+        value = sb[p, z].astype(jnp.float32)
+        for dz in range(1, nz):
+            zf = lax.rem(z + nz - dz, nz)
+            remote(sb.at[p, z], r2.at[p, dz], s2_send.at[p, dz], s2_recv.at[p, dz], (c, zf * 2 + core)).wait_recv()
+            value = value + r2[p, dz].astype(jnp.float32)
+        value = value + res_ref[:, cols].astype(jnp.float32)
+        hid_ref[:, cols] = value
+        square = square + jnp.sum(value * value, axis=-1, keepdims=True)
+    factor = lax.rsqrt(square / d_model + 1e-06)
+    full_ref[c, e] = (hid_ref[...] * factor * gain_ref[...]).astype(jnp.bfloat16)
+
+    def to_ctx(block, dz):
+        for dc in range(1, nc):
+            launch(remote(block, block, c_send.at[dz, dc], c_recv.at[dz, dc], (lax.rem(c + dc, nc), e)))
+
+    own = full_ref.at[c, e]
+    for dz in range(1, nz):
+        launch(remote(own, own, z_send.at[dz], z_recv.at[dz], (c, lax.rem(z + dz, nz) * 2 + core)))
+    to_ctx(own, 0)
+    launch(remote(own, own, p_send.at[0, 0], p_recv.at[0, 0], partner))
+    for dz in range(1, nz):
+        block = full_ref.at[c, lax.rem(z + nz - dz, nz) * 2 + core]
+        remote(block, block, z_send.at[dz], z_recv.at[dz], partner).wait_recv()
+        to_ctx(block, dz)
+        launch(remote(block, block, p_send.at[dz, 0], p_recv.at[dz, 0], partner))
+    for dz in range(nz):
+        for dc in range(1, nc):
+            block = full_ref.at[lax.rem(c + nc - dc, nc), lax.rem(z + nz - dz, nz) * 2 + core]
+            remote(block, block, c_send.at[dz, dc], c_recv.at[dz, dc], partner).wait_recv()
+            launch(remote(block, block, p_send.at[dz, dc], p_recv.at[dz, dc], partner))
+    for dz in range(nz):
+        for dc in range(nc):
+            block = full_ref.at[lax.rem(c + nc - dc, nc), lax.rem(z + nz - dz, nz) * 2 + (1 - core)]
+            remote(block, block, p_send.at[dz, dc], p_recv.at[dz, dc], partner).wait_recv()
+    for de in range(1, ne):
+        slot = routes_ref.at[lax.rem(e + ne - de, ne)]
+        remote(route_ref, slot, e_send.at[de], e_recv.at[de], partner).wait_recv()
+    for copy in sent:
+        copy.wait_send()
+
+
+def front(queries, key_rows, value_rows, w_out, residual, norm_gain, routing):
+    nc, ne = lax.axis_size("ctx"), lax.axis_size("exp")
+    tok = queries.shape[0]
+    heads = queries.shape[1] // DQK // nc
+    d_model = w_out.shape[1]
+    nz, sub = ne // 2, tok // ne
+    n_parts = parts_of(d_model)
+    width = d_model // n_parts
+    flat = routing.reshape(-1, 128)
+    vmem = pl.BlockSpec(memory_space=pltpu.VMEM)
+    dma = pltpu.SemaphoreType.DMA
+    bf16 = jnp.bfloat16
+    return pl.pallas_call(
+        functools.partial(front_kernel, nc, ne, heads),
+        out_shape=(
+            jax.ShapeDtypeStruct((sub, d_model), jnp.float32),
+            jax.ShapeDtypeStruct((nc, ne, sub, d_model), bf16),
+            jax.ShapeDtypeStruct((ne,) + flat.shape, jnp.int32),
+        ),
+        in_specs=[vmem, vmem, vmem, pl.BlockSpec(memory_space=pl.ANY), vmem, vmem, vmem],
+        out_specs=(vmem, vmem, vmem),
+        scratch_shapes=[
+            pltpu.VMEM((nc * tok, heads * DQK), bf16),
+            pltpu.VMEM((nc * tok, heads * DQK), bf16),
+            pltpu.VMEM((nc * tok, heads * DV), bf16),
+            pltpu.VMEM((nc * tok, heads * DV), bf16),
+            pltpu.VMEM((tok, nc * heads * DV), bf16),
+            pltpu.VMEM(w_out.shape, bf16),
+            pltpu.VMEM((n_parts, nz, 2, sub, width), bf16),
+            pltpu.VMEM((n_parts, nz, sub, width), bf16),
+            pltpu.VMEM((n_parts, nz, sub, width), bf16),
+            pltpu.VMEM((n_parts, nz, sub, width), bf16),
+            dma,
+            dma((3, nc)), dma((3, nc)),
+            dma((nc,)), dma((nc,)),
+            dma((ne,)), dma((ne,)),
+            dma((n_parts,)), dma((n_parts,)),
+            dma((n_parts, nz)), dma((n_parts, nz)),
+            dma((nz,)), dma((nz,)),
+            dma((nz, nc)), dma((nz, nc)),
+            dma((nz, nc)), dma((nz, nc)),
+        ],
+        compiler_params=pltpu.CompilerParams(
+            collective_id=0, has_side_effects=True, vmem_limit_bytes=56 * 1024 * 1024
+        ),
+    )(queries, key_rows, value_rows, w_out, residual, norm_gain.reshape(1, -1), flat)
+
+
+def back_kernel(
+    nc, ne, x_ref, hid_ref, out_ref, r1, sb, r2, tb, r3,
+    s1_send, s1_recv, s2_send, s2_recv, s3_send, s3_recv,
+):
+    c = lax.axis_index("ctx")
+    e = lax.axis_index("exp")
+    nz = ne // 2
+    z, core = e // 2, lax.rem(e, 2)
+    partner = (c, z * 2 + (1 - core))
+    n_parts, sub, width = r1.shape[0], r1.shape[2], r1.shape[3]
+    greet(nc, ne, c, e)
+    sent = []
+
+    def launch(copy):
+        copy.start()
+        sent.append(copy)
+
+    first = []
+    for p in range(n_parts):
+        cols = pl.ds(p * width, width)
+        copy = remote(x_ref.at[:, 1 - core, :, cols], r1.at[p], s1_send.at[p], s1_recv.at[p], partner)
+        launch(copy)
+        first.append(copy)
+    for p in range(n_parts):
+        cols = slice(p * width, (p + 1) * width)
+        first[p].wait_recv()
+        total = x_ref[:, core, :, cols].astype(jnp.float32) + r1[p].astype(jnp.float32)
+        sb[p] = total.astype(jnp.bfloat16).reshape(nc, nz, sub, width)
+        for dc in range(1, nc):
+            ct = lax.rem(c + dc, nc)
+            launch(remote(sb.at[p, ct], r2.at[p, dc], s2_send.at[p, dc], s2_recv.at[p, dc], (ct, e)))
+    for p in range(n_parts):
+        value = sb[p, c].astype(jnp.float32)
+        for dc in range(1, nc):
+            cf = lax.rem(c + nc - dc, nc)
+            remote(sb.at[p, c], r2.at[p, dc], s2_send.at[p, dc], s2_recv.at[p, dc], (cf, e)).wait_recv()
+            value = value + r2[p, dc].astype(jnp.float32)
+        tb[p] = value.astype(jnp.bfloat16)
+        for dz in range(1, nz):
+            zt = lax.rem(z + dz, nz)
+            launch(remote(tb.at[p, zt], r3.at[p, dz], s3_send.at[p, dz], s3_recv.at[p, dz], (c, zt * 2 + core)))
+    for p in range(n_parts):
+        cols = slice(p * width, (p + 1) * width)
+        value = tb[p, z].astype(jnp.float32)
+        for dz in range(1, nz):
+            zf = lax.rem(z + nz - dz, nz)
+            remote(tb.at[p, z], r3.at[p, dz], s3_send.at[p, dz], s3_recv.at[p, dz], (c, zf * 2 + core)).wait_recv()
+            value = value + r3[p, dz].astype(jnp.float32)
+        out_ref[:, cols] = (hid_ref[:, cols] + value).astype(jnp.bfloat16)
+    for copy in sent:
+        copy.wait_send()
+
+
+def back(moe_part, hidden):
+    nc, ne = lax.axis_size("ctx"), lax.axis_size("exp")
+    sub, d_model = hidden.shape
+    nz = ne // 2
+    n_parts = parts_of(d_model)
+    width = d_model // n_parts
+    vmem = pl.BlockSpec(memory_space=pltpu.VMEM)
+    dma = pltpu.SemaphoreType.DMA
+    bf16 = jnp.bfloat16
+    return pl.pallas_call(
+        functools.partial(back_kernel, nc, ne),
+        out_shape=jax.ShapeDtypeStruct((sub, d_model), bf16),
+        in_specs=[vmem, vmem],
+        out_specs=vmem,
+        scratch_shapes=[
+            pltpu.VMEM((n_parts, nc * nz, sub, width), bf16),
+            pltpu.VMEM((n_parts, nc, nz, sub, width), bf16),
+            pltpu.VMEM((n_parts, nc, nz, sub, width), bf16),
+            pltpu.VMEM((n_parts, nz, sub, width), bf16),
+            pltpu.VMEM((n_parts, nz, sub, width), bf16),
+            dma((n_parts,)), dma((n_parts,)),
+            dma((n_parts, nc)), dma((n_parts, nc)),
+            dma((n_parts, nz)), dma((n_parts, nz)),
+        ],
+        compiler_params=pltpu.CompilerParams(
+            collective_id=1, has_side_effects=True, vmem_limit_bytes=56 * 1024 * 1024
+        ),
+    )(moe_part.reshape(nc * nz, 2, sub, d_model), hidden)
+
+
+def fast_body(
+    queries, key_rows, value_rows, w_out, residual, norm_gain, router, routing, w_gate, w_up, w_down
+):
+    e = lax.axis_index("exp")
+    ne, nc = lax.axis_size("exp"), lax.axis_size("ctx")
+    top_count = routing.shape[-1]
+    sub = routing.shape[2]
+    experts = router.shape[1]
+    hidden, full, routes = front(
+        queries, key_rows, value_rows, w_out, residual, norm_gain, routing
+    )
+    d_model = hidden.shape[1]
+    group_rows = nc * sub
+    tokens = ne * group_rows
+    capacity = 3 * group_rows * top_count // (2 * experts)
+    full = full.reshape(tokens, d_model)
+    local = w_gate.shape[0]
+    listed = routes.reshape(ne, nc, sub, top_count).transpose(1, 0, 2, 3).reshape(tokens, top_count)
+    ids = jnp.arange(experts, dtype=jnp.int32)
+    named = jnp.any(listed[:, :, None] == ids[None, None, :], axis=1)
+    affinity = jax.nn.sigmoid(jnp.dot(full, router, preferred_element_type=jnp.float32))
+    chosen = jnp.where(named, affinity, 0.0)
+    weights = 2.5 * chosen / jnp.sum(chosen, axis=-1, keepdims=True)
+    here = e * local + jnp.arange(local, dtype=jnp.int32)
+    pick = (ids[:, None] == here[None, :])
+    named_here = jnp.any(listed[:, :, None] == here[None, None, :], axis=1)
+    weight_here = jnp.sum(jnp.where(pick[None], weights[:, :, None], 0.0), axis=1)
+    position = jnp.arange(tokens, dtype=jnp.int32)
+    group = position // sub % ne
+    earlier = (group[:, None] == group[None, :]) & (position[None, :] < position[:, None])
+    slot = jnp.dot(
+        earlier.astype(jnp.bfloat16), named_here.astype(jnp.bfloat16), preferred_element_type=jnp.float32
+    ).astype(jnp.int32)
+    target = jnp.where(named_here, group[:, None] * capacity + slot, -1).T
+    rows = jnp.arange(ne * capacity, dtype=jnp.int32)
+    match = target[:, None, :] == rows[None, :, None]
+    table = match.astype(jnp.bfloat16).reshape(local * ne * capacity, tokens)
+    row_weight = jnp.sum(jnp.where(match, weight_here.T[:, None, :], 0.0), axis=-1)
+    inputs = jnp.dot(table, full, preferred_element_type=jnp.float32).astype(jnp.bfloat16)
+    inputs = inputs.reshape(local, ne * capacity, d_model)
+    gate = jnp.einsum("esd,edf->esf", inputs, w_gate, preferred_element_type=jnp.float32)
+    upper = jnp.einsum("esd,edf->esf", inputs, w_up, preferred_element_type=jnp.float32)
+    expert_hidden = (jax.nn.silu(gate) * upper).astype(jnp.bfloat16)
+    outputs = jnp.einsum("esf,efd->esd", expert_hidden, w_down, preferred_element_type=jnp.float32)
+    outputs = (outputs * row_weight[..., None]).astype(jnp.bfloat16)
+    moe_part = lax.dot_general(
+        table,
+        outputs.reshape(local * ne * capacity, d_model),
+        (((0,), (0,)), ((), ())),
+        preferred_element_type=jnp.float32,
+    ).astype(jnp.bfloat16)
+    return back(moe_part, hidden)
 
 
 def from_behind(block, axis, distance):
@@ -148,4 +509,12 @@
         P("exp", "ctx", None),
     )
     out_specs = P(("ctx", "exp"), None)
-    return jax.shard_map(body, mesh=mesh, in_specs=in_specs, out_specs=out_specs, check_vma=False)
+    sizes = dict(mesh.shape)
+
+    def run(*arrays):
+        heads_here = arrays[0].shape[1] // DQK
+        rows_here = arrays[4].shape[0]
+        fits = heads_here % sizes["ctx"] == 0 and sizes["exp"] % 2 == 0 and rows_here % 16 == 0
+        return (fast_body if fits else body)(*arrays)
+
+    return jax.shard_map(run, mesh=mesh, in_specs=in_specs, out_specs=out_specs, check_vma=False)

time: 447 us -> 137 us (0.31)
  waiting for transfers between devices: 214 us -> 0 us
  blocking collectives: 134 us -> 0 us
  Pallas kernels: 0 us -> 99.9 us
  starting transfers between devices: 16.4 us -> 0 us
  between operations: 13.7 us -> 0.13 us
  local copies, waits for them, and re-layouts: 19.6 us -> 7.05 us
  other arithmetic: 13.3 us -> 0.84 us
  matrix products: 35.1 us -> 29.1 us
    all_to_all x1 -> x0, blocking collectives: 125 us -> none  [body(): lax.all_to_all(outgoing, 'exp', split_axis=0, concat_axis=0, tiled=True)]
    all_to_all x1 -> x0, waiting for transfers between devices: 121 us -> none  [body(): lax.all_to_all(partial_value, 'exp', split_axis=0, concat_axis=0, tiled=T...]
    pallas_call x0 -> x2, Pallas kernels: none -> 99.9 us  [the longest x1 66 us: front(): pl.pallas_call(functools.partial(front_kernel, nc, ne, heads), out_shape=...]
    reduce_scatter x2 -> x0, waiting for transfers between devices: 54.8 us -> none  [the longest x1 31.8 us: body(): lax.psum_scatter(jnp.dot(attended, w_out, preferred_element_type=jnp.floa...]
    ppermute x6 -> x0, waiting for transfers between devices: 38.4 us -> none  [from_behind(): return lax.ppermute(block, axis, route)]
    ppermute x6 -> x0, starting transfers between devices: 11.5 us -> none  [from_behind(): return lax.ppermute(block, axis, route)]
    gather x1 -> x0, local copies, waits for them, and re-layouts: 11.3 us -> none  [body(): jnp.take(flat_back, target, axis=0).reshape(group_rows, top_count, d_model)]
    all_gather x1 -> x0, blocking collectives: 9.75 us -> none  [body(): column = lax.all_gather(normed, 'ctx', axis=0, tiled=True)]
  transfers between devices with their start and end apart: 9 -> 0, of which waited for: 6 -> 0; matrix products, arithmetic and copies ran while one was open for 1% -> 0% of each run, Pallas kernels for 0% -> 0%
where the time goes in v1:
time: 137 us
  Pallas kernels  99.9 us (73%)
  matrix products  29.1 us (21%)
  local copies, waits for them, and re-layouts  7.05 us (5%)
    pallas_call x1, Pallas kernels, front(): pl.pallas_call(functools.partial(front_kernel, nc, ne, heads), out_shape=...  66 us
    pallas_call x1, Pallas kernels, back(): pl.pallas_call(functools.partial(back_kernel, nc, ne), out_shape=jax.Shap...  34 us
    dot_general x1, matrix products, fast_body(): lax.dot_general(table, outputs.reshape(local * ne * capacity, d_model), (...  10.6 us
    dot_general x1, matrix products, fast_body(): jnp.einsum('esd,edf->esf', inputs, w_up, preferred_element_type=jnp.float32)  8.19 us
    unnamed x10, local copies, waits for them, and re-layouts  4.04 us
    dot_general x1, matrix products, fast_body(): jnp.dot(full, router, preferred_element_type=jnp.float32)  3.5 us
    dot_general x1, matrix products, fast_body(): jnp.dot(table, full, preferred_element_type=jnp.float32)  3.48 us
    dot_general x1, matrix products, fast_body(): jnp.einsum('esd,edf->esf', inputs, w_gate, preferred_element_type=jnp.flo...  3 us

profile of v1, /device:TPU:0, one launch (start us, length us, event | category | flops | bytes accessed | tf_op | source)
XLA Modules:
  0.0 137.0 jit_solution(14110239048983936527)
XLA Ops:
  0.0 0.0 copy-start
  0.0 0.1 iota_compare_fusion.4
  0.1 1.4 reshape.138.gain_ref
  1.4 0.8 copy.20
  2.2 0.7 reshape.139.route_ref
  2.9 66.0 %shard_map.109 = (f32[16,3584]{1,0:T(8,128)}, bf16[4,8,16,3584]{3,2,1,0:T(8,128)(2,1)}, s32[8,4,128]{2,1,0:T(4,128)}) custom-call(bf16[128,1536]{1,0:T(8,128)(2,1)} %q_ref.1, bf16[128,1536]{1,0:T(8,128)(2,1)} %k_ref.1, bf16[128,1024]{1,0:T(8,128)(2,1)} %v_ref.1, bf16[1024,3584]{1,0:T(8,128)(2,1)} %w_hbm.1, bf16[16,3584]{1,0:T(8,128)(2,1)} %res_ref.1, ...), custom_call_target="tpu_custom_call" | custom-call | tf_op jit(solution)/shard_map/pallas_call | solution.py:201
  68.9 0.7 copy.21
  69.6 0.2 reshape.140
  69.8 0.1 copy.23
  69.9 0.0 copy-start.3
  69.9 0.1 compare_reduce_fusion
  70.0 0.1 fusion.12
  70.1 0.3 fusion.5
  70.4 0.0 copy-done
  70.4 3.5 %fusion.17 = (f32[512]{0:T(512)S(1)}, f32[512,32]{0,1:T(8,128)S(1)}) fusion(pred[512,32]{0,1:T(8,128)(4,1)S(1)} %fusion.12, bf16[512,3584]{1,0:T(8,128)(2,1)} %bitcast.27, bf16[3584,32]{0,1:T(8,128)(2,1)S(1)} %copy-done), kind=kOutput, calls=%fused_computation.39 | convolution fusion | flops 117521920 | bytes 3983360 | tf_op jit(solution)/shard_map/dot_general | solution.py:340
  73.9 0.1 select_reduce_fusion.1
  74.0 0.2 select_reduce_fusion
  74.3 0.2 iota_compare_fusion
  74.5 0.0 copy-done.3
  74.5 0.0 copy-start.2
  74.5 3.5 %convolution_convert_fusion = bf16[768,3584]{1,0:T(8,128)(2,1)S(1)} fusion(pred[768,512]{1,0:T(32,128)(4,1)S(1)} %bitcast.33, bf16[512,3584]{1,0:T(8,128)(2,1)S(1)} %bitcast.28), kind=kOutput, calls=%fused_computation.2 | convolution fusion | flops 2821324800 | bytes 9568256 | tf_op jit(solution)/shard_map/dot_general | solution.py:358
  78.0 1.7 %copy-done.2 = bf16[4,3584,512]{2,1,0:T(8,128)(2,1)S(1)} copy-done((bf16[4,3584,512]{2,1,0:T(8,128)(2,1)S(1)}, bf16[4,3584,512]{2,1,0:T(8,128)(2,1)}, u32[]{:S(2)}) %copy-start.2) | copy-done | bytes 14680088
  79.7 3.0 %fusion.18 = f32[4,192,512]{2,1,0:T(8,128)S(1)} fusion(bf16[4,192,3584]{2,1,0:T(8,128)(2,1)S(1)} %bitcast.29, bf16[4,3584,512]{2,1,0:T(8,128)(2,1)S(1)} %copy-done.2), kind=kOutput, calls=%fused_computation.40 | convolution fusion | flops 2818572288 | bytes 21757952 | tf_op jit(solution)/shard_map/esd,edf->esf/dot_general | solution.py:360
  82.7 8.2 %multiply_convert_fusion.1 = bf16[4,192,512]{2,1,0:T(8,128)(2,1)S(1)} fusion(f32[4,192,512]{2,1,0:T(8,128)S(1)} %fusion.18, bf16[4,192,3584]{2,1,0:T(8,128)(2,1)S(1)} %bitcast.30, bf16[4,3584,512]{2,1,0:T(8,128)(2,1)} %param.20), kind=kOutput, calls=%fused_computation.4 | convolution fusion | flops 2820931584 | bytes 22544384 | tf_op jit(solution)/shard_map/esd,edf->esf/dot_general | solution.py:361
  90.9 0.0 copy-start.1
  90.9 10.6 %bitcast_convert_fusion = bf16[512,3584]{1,0:T(8,128)(2,1)} fusion(bf16[4,192,512]{2,1,0:T(8,128)(2,1)S(1)} %multiply_convert_fusion.1, bf16[4,512,3584]{2,1,0:T(8,128)(2,1)} %param.21, f32[4,192]{1,0:T(4,128)S(1)} %select_reduce_fusion, s32[4,512]{1,0:T(4,128)S(1)} %fusion.5), kind=kOutput, calls=%fused_computation.1 | convolution fusion | flops 5644877824 | bytes 19147776 | tf_op jit(solution)/shard_map/dot_general | solution.py:365
  101.5 34.0 %shard_map.110 = bf16[16,3584]{1,0:T(8,128)(2,1)} custom-call(bf16[16,2,16,3584]{3,2,1,0:T(8,128)(2,1)} %bitcast.31, f32[16,3584]{1,0:T(8,128)} %get-tuple-element.10.hid_ref), custom_call_target="tpu_custom_call" | custom-call | tf_op jit(solution)/shard_map/pallas_call | solution.py:299
  135.5 1.6 %copy.27 = bf16[16,3584]{1,0:T(8,128)(2,1)} copy(bf16[16,3584]{1,0:T(8,128)(2,1)} %shard_map.110) | data formatting | bytes 229376
  137.0 0.0 copy-done.1
  (3 shorter events, 0.0 us)
Async XLA Ops:
  0.0 70.4 %copy-start = (bf16[3584,32]{0,1:T(8,128)(2,1)S(1)}, bf16[3584,32]{0,1:T(8,128)(2,1)}, u32[]{:S(2)}) copy-start(bf16[3584,32]{0,1:T(8,128)(2,1)} %param.17) | copy-start | bytes 688132
  69.9 4.6 %copy-start.3 = (bf16[4,8,16,3584]{3,2,1,0:T(8,128)(2,1)S(1)}, bf16[4,8,16,3584]{3,2,1,0:T(8,128)(2,1)}, u32[]{:S(2)}) copy-start(bf16[4,8,16,3584]{3,2,1,0:T(8,128)(2,1)} %get-tuple-element.9) | copy-start | bytes 11010052
  74.5 5.2 %copy-start.2 = (bf16[4,3584,512]{2,1,0:T(8,128)(2,1)S(1)}, bf16[4,3584,512]{2,1,0:T(8,128)(2,1)}, u32[]{:S(2)}) copy-start(bf16[4,3584,512]{2,1,0:T(8,128)(2,1)} %param.19) | copy-start | bytes 44040196
  90.9 46.2 %copy-start.1 = (bf16[3584,32]{0,1:T(8,128)(2,1)S(1)}, bf16[3584,32]{0,1:T(8,128)(2,1)}, u32[]{:S(2)}) copy-start(bf16[3584,32]{0,1:T(8,128)(2,1)} %param.17) | copy-start | bytes 688132

commit v2 on v1

--- a/solution.py
+++ b/solution.py
@@ -13,6 +13,8 @@
 
 NEG = -1e30
 MESH = pl.DeviceIdType.MESH
+FRONT_VMEM = 56 * 1024 * 1024
+BACK_VMEM = 56 * 1024 * 1024
 
 
 def parts_of(width):
@@ -43,12 +45,12 @@
 
 def front_kernel(
     nc, ne, heads,
-    q_ref, k_ref, v_ref, w_hbm, res_ref, gain_ref, route_ref,
-    hid_ref, full_ref, routes_ref,
+    q_ref, k_ref, v_ref, w_hbm, res_ref, gain_ref, router_ref, route_ref,
+    hid_ref, full_ref, aux_ref,
     qb, kb, vb, ab, att, wbuf, part, r1, sb, r2,
-    w_sem, a_send, a_recv, b_send, b_recv, e_send, e_recv,
+    w_sem, a_send, a_recv, b_send, b_recv,
     s1_send, s1_recv, s2_send, s2_recv,
-    z_send, z_recv, c_send, c_recv, p_send, p_recv,
+    z_send, z_recv, x_send, x_recv, y_send, y_recv, f_send, f_recv, g_send, g_recv, p_send, p_recv, q_send, q_recv,
 ):
     c = lax.axis_index("ctx")
     e = lax.axis_index("exp")
@@ -75,11 +77,6 @@
         for i, (src, buf, w) in enumerate(triples):
             cols = pl.ds(pl.multiple_of(to * w, 128), w)
             launch(remote(src.at[:, cols], buf.at[mine, :], a_send.at[i, dc], a_recv.at[i, dc], (to, e)))
-    for de in range(1, ne):
-        launch(
-            remote(route_ref, routes_ref.at[e], e_send.at[de], e_recv.at[de], (c, lax.rem(e + de, ne)))
-        )
-    routes_ref[e] = route_ref[...]
     for src, buf, w in triples:
         buf[mine, :] = src[:, pl.ds(pl.multiple_of(c * w, 128), w)]
     for dc in range(1, nc):
@@ -156,37 +153,100 @@
     factor = lax.rsqrt(square / d_model + 1e-06)
     full_ref[c, e] = (hid_ref[...] * factor * gain_ref[...]).astype(jnp.bfloat16)
 
-    def to_ctx(block, dz):
-        for dc in range(1, nc):
-            launch(remote(block, block, c_send.at[dz, dc], c_recv.at[dz, dc], (lax.rem(c + dc, nc), e)))
-
-    own = full_ref.at[c, e]
+    logits = jnp.dot(full_ref[c, e], router_ref[...], preferred_element_type=jnp.float32)
+    experts = logits.shape[1]
+    affinity = jnp.concatenate([jax.nn.sigmoid(logits)] * 4, axis=1)
+    lane = lax.broadcasted_iota(jnp.int32, affinity.shape, 1)
+    listed = route_ref[0, c]
+    named = jnp.zeros(affinity.shape, jnp.float32)
+    for k in range(listed.shape[1]):
+        named = jnp.where(listed[:, k : k + 1] == lax.rem(lane, experts), 1.0, named)
+    chosen = jnp.where(named > 0.0, affinity, 0.0)
+    whole = jnp.sum(jnp.where(lane < experts, chosen, 0.0), axis=-1, keepdims=True)
+    weight = 2.5 * chosen / whole
+    high = weight.astype(jnp.bfloat16).astype(jnp.float32)
+    middle = (weight - high).astype(jnp.bfloat16).astype(jnp.float32)
+    low = weight - high - middle
+    packed = jnp.where(lane < experts, high, jnp.where(lane < 2 * experts, middle, low))
+    aux_ref[c, e] = jnp.where(lane < 3 * experts, packed, named).astype(jnp.bfloat16)
+
+    ny = nc // 2
+    y, x = c // 2, lax.rem(c, 2)
+    beside = (y * 2 + (1 - x), e)
+    half = full_ref.shape[-1] // 2
+    sets = (full_ref, aux_ref)
+
+    def above(dy):
+        return lax.rem(y + dy, ny) * 2 + x
+
+    def below(dy):
+        return lax.rem(y + ny - dy, ny) * 2 + x
+
+    def origin(dz, k):
+        return lax.rem(z + nz - dz, nz) * 2 + k
+
+    def moves(ctx_from, exp_from, send, recv, index, device):
+        return [
+            remote(ref.at[ctx_from, exp_from], ref.at[ctx_from, exp_from], send.at[(i,) + index], recv.at[(i,) + index], device)
+            for i, ref in enumerate(sets)
+        ]
+
+    def relays(ctx_from, exp_from, part_no, send, recv, index, device):
+        block = full_ref.at[ctx_from, exp_from, :, pl.ds(part_no * half, half)]
+        out = [remote(block, block, send.at[(0,) + index], recv.at[(0,) + index], device)]
+        if part_no == 0:
+            side = aux_ref.at[ctx_from, exp_from]
+            out.append(remote(side, side, send.at[(1,) + index], recv.at[(1,) + index], device))
+        return out
+
+    def launch_all(copies):
+        for copy in copies:
+            launch(copy)
+
+    def arrive(copies):
+        for copy in copies:
+            copy.wait_recv()
+
+    def spread(dz):
+        who = origin(dz, core)
+        launch_all(moves(c, who, x_send, x_recv, (dz,), beside))
+        for dy in range(1, ny):
+            launch_all(moves(c, who, y_send, y_recv, (dz, dy), (above(dy), e)))
+        launch_all(moves(c, who, p_send, p_recv, (dz, 0), partner))
+
     for dz in range(1, nz):
-        launch(remote(own, own, z_send.at[dz], z_recv.at[dz], (c, lax.rem(z + dz, nz) * 2 + core)))
-    to_ctx(own, 0)
-    launch(remote(own, own, p_send.at[0, 0], p_recv.at[0, 0], partner))
+        launch_all(moves(c, e, z_send, z_recv, (dz,), (c, lax.rem(z + dz, nz) * 2 + core)))
+    spread(0)
     for dz in range(1, nz):
-        block = full_ref.at[c, lax.rem(z + nz - dz, nz) * 2 + core]
-        remote(block, block, z_send.at[dz], z_recv.at[dz], partner).wait_recv()
-        to_ctx(block, dz)
-        launch(remote(block, block, p_send.at[dz, 0], p_recv.at[dz, 0], partner))
+        arrive(moves(c, origin(dz, core), z_send, z_recv, (dz,), partner))
+        spread(dz)
     for dz in range(nz):
-        for dc in range(1, nc):
-            block = full_ref.at[lax.rem(c + nc - dc, nc), lax.rem(z + nz - dz, nz) * 2 + core]
-            remote(block, block, c_send.at[dz, dc], c_recv.at[dz, dc], partner).wait_recv()
-            launch(remote(block, block, p_send.at[dz, dc], p_recv.at[dz, dc], partner))
+        who = origin(dz, core)
+        arrive(moves(beside[0], who, x_send, x_recv, (dz,), beside))
+        for dy in range(1, ny):
+            launch_all(relays(beside[0], who, 1, g_send, g_recv, (dz, dy), (above(dy), e)))
+        for dy in range(1, ny):
+            arrive(moves(below(dy), who, y_send, y_recv, (dz, dy), beside))
+            launch_all(relays(below(dy), who, 0, f_send, f_recv, (dz, dy), beside))
+            launch_all(moves(below(dy), who, p_send, p_recv, (dz, dy), partner))
+        launch_all(moves(beside[0], who, q_send, q_recv, (dz, 0), partner))
     for dz in range(nz):
-        for dc in range(nc):
-            block = full_ref.at[lax.rem(c + nc - dc, nc), lax.rem(z + nz - dz, nz) * 2 + (1 - core)]
-            remote(block, block, p_send.at[dz, dc], p_recv.at[dz, dc], partner).wait_recv()
-    for de in range(1, ne):
-        slot = routes_ref.at[lax.rem(e + ne - de, ne)]
-        remote(route_ref, slot, e_send.at[de], e_recv.at[de], partner).wait_recv()
+        who = origin(dz, core)
+        for dy in range(1, ny):
+            corner = below(dy) - x + (1 - x)
+            arrive(relays(corner, who, 0, f_send, f_recv, (dz, dy), beside))
+            arrive(relays(corner, who, 1, g_send, g_recv, (dz, dy), beside))
+            launch_all(moves(corner, who, q_send, q_recv, (dz, dy), partner))
+    for dz in range(nz):
+        who = origin(dz, 1 - core)
+        for dy in range(ny):
+            arrive(moves(below(dy), who, p_send, p_recv, (dz, dy), partner))
+            arrive(moves(below(dy) - x + (1 - x), who, q_send, q_recv, (dz, dy), partner))
     for copy in sent:
         copy.wait_send()
 
 
-def front(queries, key_rows, value_rows, w_out, residual, norm_gain, routing):
+def front(queries, key_rows, value_rows, w_out, residual, norm_gain, router, routing):
     nc, ne = lax.axis_size("ctx"), lax.axis_size("exp")
     tok = queries.shape[0]
     heads = queries.shape[1] // DQK // nc
@@ -194,7 +254,7 @@
     nz, sub = ne // 2, tok // ne
     n_parts = parts_of(d_model)
     width = d_model // n_parts
-    flat = routing.reshape(-1, 128)
+    ny = nc // 2
     vmem = pl.BlockSpec(memory_space=pltpu.VMEM)
     dma = pltpu.SemaphoreType.DMA
     bf16 = jnp.bfloat16
@@ -203,9 +263,9 @@
         out_shape=(
             jax.ShapeDtypeStruct((sub, d_model), jnp.float32),
             jax.ShapeDtypeStruct((nc, ne, sub, d_model), bf16),
-            jax.ShapeDtypeStruct((ne,) + flat.shape, jnp.int32),
+            jax.ShapeDtypeStruct((nc, ne, sub, 4 * router.shape[1]), bf16),
         ),
-        in_specs=[vmem, vmem, vmem, pl.BlockSpec(memory_space=pl.ANY), vmem, vmem, vmem],
+        in_specs=[vmem, vmem, vmem, pl.BlockSpec(memory_space=pl.ANY), vmem, vmem, vmem, vmem],
         out_specs=(vmem, vmem, vmem),
         scratch_shapes=[
             pltpu.VMEM((nc * tok, heads * DQK), bf16),
@@ -221,29 +281,34 @@
             dma,
             dma((3, nc)), dma((3, nc)),
             dma((nc,)), dma((nc,)),
-            dma((ne,)), dma((ne,)),
             dma((n_parts,)), dma((n_parts,)),
             dma((n_parts, nz)), dma((n_parts, nz)),
-            dma((nz,)), dma((nz,)),
-            dma((nz, nc)), dma((nz, nc)),
-            dma((nz, nc)), dma((nz, nc)),
+            dma((2, nz)), dma((2, nz)),
+            dma((2, nz)), dma((2, nz)),
+            dma((2, nz, ny)), dma((2, nz, ny)),
+            dma((2, nz, ny)), dma((2, nz, ny)),
+            dma((2, nz, ny)), dma((2, nz, ny)),
+            dma((2, nz, ny)), dma((2, nz, ny)),
+            dma((2, nz, ny)), dma((2, nz, ny)),
         ],
         compiler_params=pltpu.CompilerParams(
-            collective_id=0, has_side_effects=True, vmem_limit_bytes=56 * 1024 * 1024
+            collective_id=0, has_side_effects=True, vmem_limit_bytes=FRONT_VMEM
         ),
-    )(queries, key_rows, value_rows, w_out, residual, norm_gain.reshape(1, -1), flat)
+    )(queries, key_rows, value_rows, w_out, residual, norm_gain.reshape(1, -1), router, routing)
 
 
 def back_kernel(
-    nc, ne, x_ref, hid_ref, out_ref, r1, sb, r2, tb, r3,
-    s1_send, s1_recv, s2_send, s2_recv, s3_send, s3_recv,
+    nc, ne, x_ref, out_ref, r1, sb, rx, ux, ry, tb, r3,
+    s1_send, s1_recv, x_send, x_recv, y_send, y_recv, s3_send, s3_recv,
 ):
     c = lax.axis_index("ctx")
     e = lax.axis_index("exp")
-    nz = ne // 2
+    nz, ny = ne // 2, nc // 2
     z, core = e // 2, lax.rem(e, 2)
+    y, x = c // 2, lax.rem(c, 2)
     partner = (c, z * 2 + (1 - core))
-    n_parts, sub, width = r1.shape[0], r1.shape[2], r1.shape[3]
+    beside = (y * 2 + (1 - x), e)
+    n_parts, sub, width = r1.shape[0], r1.shape[4], r1.shape[5]
     greet(nc, ne, c, e)
     sent = []
 
@@ -251,38 +316,63 @@
         copy.start()
         sent.append(copy)
 
+    def ctx_at(row):
+        return (row * 2 + x, e)
+
+    def wide(ref):
+        return ref.astype(jnp.float32)
+
     first = []
     for p in range(n_parts):
         cols = pl.ds(p * width, width)
-        copy = remote(x_ref.at[:, 1 - core, :, cols], r1.at[p], s1_send.at[p], s1_recv.at[p], partner)
+        copy = remote(x_ref.at[:, :, :, 1 - core, :, cols], r1.at[p], s1_send.at[p], s1_recv.at[p], partner)
         launch(copy)
         first.append(copy)
     for p in range(n_parts):
         cols = slice(p * width, (p + 1) * width)
         first[p].wait_recv()
-        total = x_ref[:, core, :, cols].astype(jnp.float32) + r1[p].astype(jnp.float32)
-        sb[p] = total.astype(jnp.bfloat16).reshape(nc, nz, sub, width)
-        for dc in range(1, nc):
-            ct = lax.rem(c + dc, nc)
-            launch(remote(sb.at[p, ct], r2.at[p, dc], s2_send.at[p, dc], s2_recv.at[p, dc], (ct, e)))
-    for p in range(n_parts):
-        value = sb[p, c].astype(jnp.float32)
-        for dc in range(1, nc):
-            cf = lax.rem(c + nc - dc, nc)
-            remote(sb.at[p, c], r2.at[p, dc], s2_send.at[p, dc], s2_recv.at[p, dc], (cf, e)).wait_recv()
-            value = value + r2[p, dc].astype(jnp.float32)
+        sb[p] = (wide(x_ref[:, :, :, core, :, cols]) + wide(r1[p])).astype(jnp.bfloat16)
+        if p % 2 == 0:
+            launch(remote(sb.at[p, :, 1 - x], rx.at[p], x_send.at[p], x_recv.at[p], beside))
+        else:
+            for dy in range(1, ny):
+                yt = lax.rem(y + dy, ny)
+                launch(remote(sb.at[p, yt], ry.at[p, dy], y_send.at[p, dy], y_recv.at[p, dy], ctx_at(yt)))
+    for p in range(n_parts):
+        if p % 2 == 0:
+            remote(sb.at[p, :, 1 - x], rx.at[p], x_send.at[p], x_recv.at[p], beside).wait_recv()
+            ux[p] = (wide(sb[p, :, x]) + wide(rx[p])).astype(jnp.bfloat16)
+            for dy in range(1, ny):
+                yt = lax.rem(y + dy, ny)
+                launch(remote(ux.at[p, yt], ry.at[p, dy, 0], y_send.at[p, dy], y_recv.at[p, dy], ctx_at(yt)))
+        else:
+            value = wide(sb[p, y])
+            for dy in range(1, ny):
+                remote(sb.at[p, y], ry.at[p, dy], y_send.at[p, dy], y_recv.at[p, dy], ctx_at(lax.rem(y + ny - dy, ny))).wait_recv()
+                value = value + wide(ry[p, dy])
+            ux[p, 0:2] = value.astype(jnp.bfloat16)
+            launch(remote(ux.at[p, 1 - x], rx.at[p, 0], x_send.at[p], x_recv.at[p], beside))
+    for p in range(n_parts):
+        if p % 2 == 0:
+            value = wide(ux[p, y])
+            for dy in range(1, ny):
+                remote(ux.at[p, y], ry.at[p, dy, 0], y_send.at[p, dy], y_recv.at[p, dy], ctx_at(lax.rem(y + ny - dy, ny))).wait_recv()
+                value = value + wide(ry[p, dy, 0])
+        else:
+            remote(ux.at[p, 1 - x], rx.at[p, 0], x_send.at[p], x_recv.at[p], beside).wait_recv()
+            value = wide(ux[p, x]) + wide(rx[p, 0])
         tb[p] = value.astype(jnp.bfloat16)
         for dz in range(1, nz):
             zt = lax.rem(z + dz, nz)
             launch(remote(tb.at[p, zt], r3.at[p, dz], s3_send.at[p, dz], s3_recv.at[p, dz], (c, zt * 2 + core)))
     for p in range(n_parts):
         cols = slice(p * width, (p + 1) * width)
-        value = tb[p, z].astype(jnp.float32)
+        value = wide(tb[p, z])
         for dz in range(1, nz):
             zf = lax.rem(z + nz - dz, nz)
             remote(tb.at[p, z], r3.at[p, dz], s3_send.at[p, dz], s3_recv.at[p, dz], (c, zf * 2 + core)).wait_recv()
-            value = value + r3[p, dz].astype(jnp.float32)
-        out_ref[:, cols] = (hid_ref[:, cols] + value).astype(jnp.bfloat16)
+            value = value + wide(r3[p, dz])
+        out_ref[:, cols] = value
     for copy in sent:
         copy.wait_send()
 
@@ -290,31 +380,34 @@
 def back(moe_part, hidden):
     nc, ne = lax.axis_size("ctx"), lax.axis_size("exp")
     sub, d_model = hidden.shape
-    nz = ne // 2
-    n_parts = parts_of(d_model)
+    nz, ny = ne // 2, nc // 2
+    n_parts = 4 if d_model % 512 == 0 else 2
     width = d_model // n_parts
     vmem = pl.BlockSpec(memory_space=pltpu.VMEM)
     dma = pltpu.SemaphoreType.DMA
     bf16 = jnp.bfloat16
     return pl.pallas_call(
         functools.partial(back_kernel, nc, ne),
-        out_shape=jax.ShapeDtypeStruct((sub, d_model), bf16),
-        in_specs=[vmem, vmem],
+        out_shape=jax.ShapeDtypeStruct((sub, d_model), jnp.float32),
+        in_specs=[vmem],
         out_specs=vmem,
         scratch_shapes=[
-            pltpu.VMEM((n_parts, nc * nz, sub, width), bf16),
-            pltpu.VMEM((n_parts, nc, nz, sub, width), bf16),
-            pltpu.VMEM((n_parts, nc, nz, sub, width), bf16),
+            pltpu.VMEM((n_parts, ny, 2, nz, sub, width), bf16),
+            pltpu.VMEM((n_parts, ny, 2, nz, sub, width), bf16),
+            pltpu.VMEM((n_parts, ny, nz, sub, width), bf16),
+            pltpu.VMEM((n_parts, max(ny, 2), nz, sub, width), bf16),
+            pltpu.VMEM((n_parts, ny, 2, nz, sub, width), bf16),
             pltpu.VMEM((n_parts, nz, sub, width), bf16),
             pltpu.VMEM((n_parts, nz, sub, width), bf16),
             dma((n_parts,)), dma((n_parts,)),
-            dma((n_parts, nc)), dma((n_parts, nc)),
+            dma((n_parts,)), dma((n_parts,)),
+            dma((n_parts, ny)), dma((n_parts, ny)),
             dma((n_parts, nz)), dma((n_parts, nz)),
         ],
         compiler_params=pltpu.CompilerParams(
-            collective_id=1, has_side_effects=True, vmem_limit_bytes=56 * 1024 * 1024
+            collective_id=1, has_side_effects=True, vmem_limit_bytes=BACK_VMEM
         ),
-    )(moe_part.reshape(nc * nz, 2, sub, d_model), hidden)
+    )(moe_part.reshape(ny, 2, nz, 2, sub, d_model))
 
 
 def fast_body(
@@ -325,8 +418,8 @@
     top_count = routing.shape[-1]
     sub = routing.shape[2]
     experts = router.shape[1]
-    hidden, full, routes = front(
-        queries, key_rows, value_rows, w_out, residual, norm_gain, routing
+    hidden, full, aux = front(
+        queries, key_rows, value_rows, w_out, residual, norm_gain, router, routing
     )
     d_model = hidden.shape[1]
     group_rows = nc * sub
@@ -334,16 +427,14 @@
     capacity = 3 * group_rows * top_count // (2 * experts)
     full = full.reshape(tokens, d_model)
     local = w_gate.shape[0]
-    listed = routes.reshape(ne, nc, sub, top_count).transpose(1, 0, 2, 3).reshape(tokens, top_count)
-    ids = jnp.arange(experts, dtype=jnp.int32)
-    named = jnp.any(listed[:, :, None] == ids[None, None, :], axis=1)
-    affinity = jax.nn.sigmoid(jnp.dot(full, router, preferred_element_type=jnp.float32))
-    chosen = jnp.where(named, affinity, 0.0)
-    weights = 2.5 * chosen / jnp.sum(chosen, axis=-1, keepdims=True)
-    here = e * local + jnp.arange(local, dtype=jnp.int32)
-    pick = (ids[:, None] == here[None, :])
-    named_here = jnp.any(listed[:, :, None] == here[None, None, :], axis=1)
-    weight_here = jnp.sum(jnp.where(pick[None], weights[:, :, None], 0.0), axis=1)
+    lanes = jnp.arange(4 * experts, dtype=jnp.int32)[:, None]
+    here = e * local + jnp.arange(local, dtype=jnp.int32)[None, :]
+    pick = lanes % experts == here
+    pick = jnp.concatenate([pick & (lanes < 3 * experts), pick & (lanes >= 3 * experts)], axis=1)
+    mine = jnp.dot(
+        aux.reshape(tokens, 4 * experts), pick.astype(jnp.bfloat16), preferred_element_type=jnp.float32
+    )
+    weight_here, named_here = mine[:, :local], mine[:, local:] > 0.5
     position = jnp.arange(tokens, dtype=jnp.int32)
     group = position // sub % ne
     earlier = (group[:, None] == group[None, :]) & (position[None, :] < position[:, None])
@@ -368,7 +459,7 @@
         (((0,), (0,)), ((), ())),
         preferred_element_type=jnp.float32,
     ).astype(jnp.bfloat16)
-    return back(moe_part, hidden)
+    return (hidden + back(moe_part, hidden)).astype(jnp.bfloat16)
 
 
 def from_behind(block, axis, distance):
@@ -514,7 +605,7 @@
     def run(*arrays):
         heads_here = arrays[0].shape[1] // DQK
         rows_here = arrays[4].shape[0]
-        fits = heads_here % sizes["ctx"] == 0 and sizes["exp"] % 2 == 0 and rows_here % 16 == 0
+        fits = heads_here % sizes["ctx"] == 0 and sizes["ctx"] % 2 == 0 and sizes["exp"] % 2 == 0 and rows_here % 16 == 0
         return (fast_body if fits else body)(*arrays)
 
     return jax.shard_map(run, mesh=mesh, in_specs=in_specs, out_specs=out_specs, check_vma=False)

time: 137 us -> 140 us (1.022)
  Pallas kernels: 99.9 us -> 103 us
  local copies, waits for them, and re-layouts: 7.05 us -> 4.94 us
    dot_general x1, matrix products: 3.5 us -> 1.04 us  [fast_body(): jnp.dot(aux.reshape(tokens, 4 * experts), pick.astype(jnp.bfloat16), pref...]
    dot_general x1, matrix products: 3.48 us -> 5.6 us  [fast_body(): jnp.dot(table, full, preferred_element_type=jnp.float32)]
    pallas_call x1, Pallas kernels: 34 us -> 36 us  [back(): pl.pallas_call(functools.partial(back_kernel, nc, ne), out_shape=jax.Shap...]
    convert_element_type x0 -> x1, other arithmetic: none -> 1.61 us  [fast_body(): return (hidden + back(moe_part, hidden)).astype(jnp.bfloat16)]
    unnamed x10 -> x12, local copies, waits for them, and re-layouts: 4.04 us -> 3.62 us
where the time goes in v2:
time: 140 us; the launch traced here: 139 us
  Pallas kernels  103 us (74%)
  matrix products  28.8 us (21%)
  local copies, waits for them, and re-layouts  4.94 us (4%)
  other arithmetic  2.16 us (2%)
    pallas_call x1, Pallas kernels, front(): pl.pallas_call(functools.partial(front_kernel, nc, ne, heads), out_shape=...  67.2 us
    pallas_call x1, Pallas kernels, back(): pl.pallas_call(functools.partial(back_kernel, nc, ne), out_shape=jax.Shap...  36 us
    dot_general x1, matrix products, fast_body(): lax.dot_general(table, outputs.reshape(local * ne * capacity, d_model), (...  10.5 us
    dot_general x1, matrix products, fast_body(): jnp.einsum('esd,edf->esf', inputs, w_up, preferred_element_type=jnp.float32)  8.25 us
    dot_general x1, matrix products, fast_body(): jnp.dot(table, full, preferred_element_type=jnp.float32)  5.6 us
    unnamed x12, local copies, waits for them, and re-layouts  3.62 us
    dot_general x1, matrix products, fast_body(): jnp.einsum('esd,edf->esf', inputs, w_gate, preferred_element_type=jnp.flo...  3 us

profile of v2, /device:TPU:0, one launch (start us, length us, event | category | flops | bytes accessed | tf_op | source)
XLA Modules:
  0.0 139.2 jit_solution(14122061818681188852)
XLA Ops:
  0.0 0.1 compare_and_fusion.1
  0.1 1.3 reshape.134.gain_ref
  1.4 1.4 %copy.15.route_ref = s32[1,4,16,8]{3,2,1,0:T(8,128)} copy(s32[1,4,16,8]{2,3,1,0:T(8,128)} %param.18) | data formatting | bytes 4096 | tf_op args[7]
  2.8 2.2 %copy.14.router_ref = bf16[3584,32]{1,0:T(8,128)(2,1)} copy(bf16[3584,32]{0,1:T(8,128)(2,1)} %param.17) | data formatting | bytes 458752 | tf_op args[6]
  5.0 0.0 slice-start
  5.0 0.0 slice-start.1
  5.0 67.2 %shard_map.109 = (f32[16,3584]{1,0:T(8,128)}, bf16[4,8,16,3584]{3,2,1,0:T(8,128)(2,1)}, bf16[4,8,16,128]{3,2,1,0:T(8,128)(2,1)}) custom-call(bf16[128,1536]{1,0:T(8,128)(2,1)} %q_ref.1, bf16[128,1536]{1,0:T(8,128)(2,1)} %k_ref.1, bf16[128,1024]{1,0:T(8,128)(2,1)} %v_ref.1, bf16[1024,3584]{1,0:T(8,128)(2,1)} %w_hbm.1, bf16[16,3584]{1,0:T(8,128)(2,1)} %res_ref.1, ...), custom_call_target="tpu_custom_call" | custom-call | tf_op jit(solution)/shard_map/pallas_call | solution.py:261
  72.3 1.0 fusion.10
  73.3 0.3 fusion.2
  73.7 0.2 select_reduce_fusion
  73.9 0.2 iota_compare_fusion
  74.1 0.0 slice-start.2
  74.1 0.0 slice-start.3
  74.1 5.6 %convolution_convert_fusion = bf16[768,3584]{1,0:T(8,128)(2,1)S(1)} fusion(pred[768,512]{1,0:T(32,128)(4,1)S(1)} %bitcast.25, bf16[512,3584]{1,0:T(8,128)(2,1)} %bitcast.27), kind=kOutput, calls=%fused_computation.2 | convolution fusion | flops 2821324800 | bytes 9568256 | tf_op jit(solution)/shard_map/dot_general | solution.py:449
  79.8 0.0 slice-done
  79.8 0.0 slice-done.1
  79.8 0.0 slice-done.2
  79.8 0.0 slice-done.3
  79.8 3.0 %fusion.20 = f32[4,192,512]{2,1,0:T(8,128)S(1)} fusion(bf16[4,192,3584]{2,1,0:T(8,128)(2,1)S(1)} %bitcast.22, bf16[4,3584,512]{2,1,0:T(8,128)(2,1)S(1)} %bitcast.21), kind=kOutput, calls=%fused_computation.44 | convolution fusion | flops 2818572288 | bytes 21757952 | tf_op jit(solution)/shard_map/esd,edf->esf/dot_general | solution.py:451
  82.8 8.3 %multiply_convert_fusion.1 = bf16[4,192,512]{2,1,0:T(8,128)(2,1)S(1)} fusion(f32[4,192,512]{2,1,0:T(8,128)S(1)} %fusion.20, bf16[4,192,3584]{2,1,0:T(8,128)(2,1)S(1)} %bitcast.23, bf16[4,3584,512]{2,1,0:T(8,128)(2,1)} %param.20), kind=kOutput, calls=%fused_computation.4 | convolution fusion | flops 2820931584 | bytes 22544384 | tf_op jit(solution)/shard_map/esd,edf->esf/dot_general | solution.py:452
  91.1 0.0 copy-start
  91.1 10.5 %bitcast_convert_fusion = bf16[512,3584]{1,0:T(8,128)(2,1)} fusion(bf16[4,192,512]{2,1,0:T(8,128)(2,1)S(1)} %multiply_convert_fusion.1, bf16[4,512,3584]{2,1,0:T(8,128)(2,1)} %param.21, f32[4,192]{1,0:T(4,128)S(1)} %select_reduce_fusion, s32[4,512]{1,0:T(4,128)S(1)} %fusion.2), kind=kOutput, calls=%fused_computation.1 | convolution fusion | flops 5644877824 | bytes 19147776 | tf_op jit(solution)/shard_map/dot_general | solution.py:456
  101.6 36.0 %shard_map.110 = f32[16,3584]{1,0:T(8,128)} custom-call(bf16[2,2,4,2,16,3584]{5,4,3,2,1,0:T(8,128)(2,1)} %bitcast.24), custom_call_target="tpu_custom_call" | custom-call | tf_op jit(solution)/shard_map/pallas_call | solution.py:389
  137.6 0.0 copy-done
  137.6 1.6 %add_convert_fusion = bf16[16,3584]{1,0:T(8,128)(2,1)} fusion(f32[16,3584]{1,0:T(8,128)S(1)} %copy-done, f32[16,3584]{1,0:T(8,128)} %shard_map.110), kind=kLoop, calls=%fused_computation.16 | loop fusion | flops 114688 | bytes 573440 | tf_op jit(solution)/shard_map/convert_element_type | solution.py:462
  (6 shorter events, 0.0 us)
Async XLA Ops:
  5.0 74.7 %slice-start = ((s8[14680064]{0:T(1024)(128)(4,1)}), s8[4194304]{0:T(1024)(128)(4,1)S(1)}, s32[]{:S(2)}) async-start(s8[14680064]{0:T(1024)(128)(4,1)} %bitcast.20), calls=%async_computation | async-start | bytes 8388608
  5.0 74.8 %slice-start.1 = ((s8[14680064]{0:T(1024)(128)(4,1)}), s8[2097152]{0:T(1024)(128)(4,1)S(1)}, s32[]{:S(2)}) async-start(s8[14680064]{0:T(1024)(128)(4,1)} %bitcast.20), calls=%async_computation.1 | async-start | bytes 4194304
  74.1 5.7 %slice-start.2 = ((s8[14680064]{0:T(1024)(128)(4,1)}), s8[4194304]{0:T(1024)(128)(4,1)S(1)}, s32[]{:S(2)}) async-start(s8[14680064]{0:T(1024)(128)(4,1)} %bitcast.20), calls=%async_computation.2 | async-start | bytes 8388608
  74.1 5.7 %slice-start.3 = ((s8[14680064]{0:T(1024)(128)(4,1)}), s8[4194304]{0:T(1024)(128)(4,1)S(1)}, s32[]{:S(2)}) async-start(s8[14680064]{0:T(1024)(128)(4,1)} %bitcast.20), calls=%async_computation.3 | async-start | bytes 8388608
  91.1 46.5 %copy-start = (f32[16,3584]{1,0:T(8,128)S(1)}, f32[16,3584]{1,0:T(8,128)}, u32[]{:S(2)}) copy-start(f32[16,3584]{1,0:T(8,128)} %get-tuple-element.8) | copy-start | bytes 688132

commit v3 on v2

--- a/solution.py
+++ b/solution.py
@@ -128,17 +128,22 @@
             back.wait()
 
     sub = tok // ne
+    def pair_sum(p):
+        remote(part.at[p, :, 1 - core], r1.at[p], s1_send.at[p], s1_recv.at[p], partner).wait_recv()
+        sb[p] = (part[p, :, core].astype(jnp.float32) + r1[p].astype(jnp.float32)).astype(jnp.bfloat16)
+        for dz in range(1, nz):
+            zt = lax.rem(z + dz, nz)
+            launch(remote(sb.at[p, zt], r2.at[p, dz], s2_send.at[p, dz], s2_recv.at[p, dz], (c, zt * 2 + core)))
+
     for p in range(n_parts):
         cols = slice(p * width, (p + 1) * width)
         term = jnp.dot(att[...], wbuf[:, cols], preferred_element_type=jnp.float32)
         part[p] = term.astype(jnp.bfloat16).reshape(nz, 2, sub, width)
         launch(remote(part.at[p, :, 1 - core], r1.at[p], s1_send.at[p], s1_recv.at[p], partner))
-    for p in range(n_parts):
-        remote(part.at[p, :, 1 - core], r1.at[p], s1_send.at[p], s1_recv.at[p], partner).wait_recv()
-        sb[p] = (part[p, :, core].astype(jnp.float32) + r1[p].astype(jnp.float32)).astype(jnp.bfloat16)
-        for dz in range(1, nz):
-            zt = lax.rem(z + dz, nz)
-            launch(remote(sb.at[p, zt], r2.at[p, dz], s2_send.at[p, dz], s2_recv.at[p, dz], (c, zt * 2 + core)))
+        if p >= 2:
+            pair_sum(p - 2)
+    for p in range(max(n_parts - 2, 0), n_parts):
+        pair_sum(p)
     square = jnp.zeros((sub, 1), jnp.float32)
     for p in range(n_parts):
         cols = slice(p * width, (p + 1) * width)
@@ -153,11 +158,13 @@
     factor = lax.rsqrt(square / d_model + 1e-06)
     full_ref[c, e] = (hid_ref[...] * factor * gain_ref[...]).astype(jnp.bfloat16)
 
-    logits = jnp.dot(full_ref[c, e], router_ref[...], preferred_element_type=jnp.float32)
+    logits = lax.dot_general(
+        full_ref[c, e], router_ref[...], (((1,), (1,)), ((), ())), preferred_element_type=jnp.float32
+    )
     experts = logits.shape[1]
     affinity = jnp.concatenate([jax.nn.sigmoid(logits)] * 4, axis=1)
     lane = lax.broadcasted_iota(jnp.int32, affinity.shape, 1)
-    listed = route_ref[0, c]
+    listed = route_ref[0, c].astype(jnp.float32).T.astype(jnp.int32)
     named = jnp.zeros(affinity.shape, jnp.float32)
     for k in range(listed.shape[1]):
         named = jnp.where(listed[:, k : k + 1] == lax.rem(lane, experts), 1.0, named)
@@ -294,21 +301,19 @@
         compiler_params=pltpu.CompilerParams(
             collective_id=0, has_side_effects=True, vmem_limit_bytes=FRONT_VMEM
         ),
-    )(queries, key_rows, value_rows, w_out, residual, norm_gain.reshape(1, -1), router, routing)
+    )(queries, key_rows, value_rows, w_out, residual, norm_gain.reshape(1, -1), router.T, routing.transpose(0, 1, 3, 2))
 
 
 def back_kernel(
-    nc, ne, x_ref, out_ref, r1, sb, rx, ux, ry, tb, r3,
-    s1_send, s1_recv, x_send, x_recv, y_send, y_recv, s3_send, s3_recv,
+    nc, ne, x_ref, out_ref, r1, sb, r2, tb, r3,
+    s1_send, s1_recv, s2_send, s2_recv, s3_send, s3_recv,
 ):
     c = lax.axis_index("ctx")
     e = lax.axis_index("exp")
-    nz, ny = ne // 2, nc // 2
+    nz = ne // 2
     z, core = e // 2, lax.rem(e, 2)
-    y, x = c // 2, lax.rem(c, 2)
     partner = (c, z * 2 + (1 - core))
-    beside = (y * 2 + (1 - x), e)
-    n_parts, sub, width = r1.shape[0], r1.shape[4], r1.shape[5]
+    n_parts, sub, width = r1.shape[0], r1.shape[2], r1.shape[3]
     greet(nc, ne, c, e)
     sent = []
 
@@ -316,63 +321,50 @@
         copy.start()
         sent.append(copy)
 
-    def ctx_at(row):
-        return (row * 2 + x, e)
-
-    def wide(ref):
-        return ref.astype(jnp.float32)
-
     first = []
     for p in range(n_parts):
         cols = pl.ds(p * width, width)
-        copy = remote(x_ref.at[:, :, :, 1 - core, :, cols], r1.at[p], s1_send.at[p], s1_recv.at[p], partner)
+        copy = remote(x_ref.at[:, 1 - core, :, cols], r1.at[p], s1_send.at[p], s1_recv.at[p], partner)
         launch(copy)
         first.append(copy)
-    for p in range(n_parts):
+    def stage_two(p):
         cols = slice(p * width, (p + 1) * width)
         first[p].wait_recv()
-        sb[p] = (wide(x_ref[:, :, :, core, :, cols]) + wide(r1[p])).astype(jnp.bfloat16)
-        if p % 2 == 0:
-            launch(remote(sb.at[p, :, 1 - x], rx.at[p], x_send.at[p], x_recv.at[p], beside))
-        else:
-            for dy in range(1, ny):
-                yt = lax.rem(y + dy, ny)
-                launch(remote(sb.at[p, yt], ry.at[p, dy], y_send.at[p, dy], y_recv.at[p, dy], ctx_at(yt)))
-    for p in range(n_parts):
-        if p % 2 == 0:
-            remote(sb.at[p, :, 1 - x], rx.at[p], x_send.at[p], x_recv.at[p], beside).wait_recv()
-            ux[p] = (wide(sb[p, :, x]) + wide(rx[p])).astype(jnp.bfloat16)
-            for dy in range(1, ny):
-                yt = lax.rem(y + dy, ny)
-                launch(remote(ux.at[p, yt], ry.at[p, dy, 0], y_send.at[p, dy], y_recv.at[p, dy], ctx_at(yt)))
-        else:
-            value = wide(sb[p, y])
-            for dy in range(1, ny):
-                remote(sb.at[p, y], ry.at[p, dy], y_send.at[p, dy], y_recv.at[p, dy], ctx_at(lax.rem(y + ny - dy, ny))).wait_recv()
-                value = value + wide(ry[p, dy])
-            ux[p, 0:2] = value.astype(jnp.bfloat16)
-            launch(remote(ux.at[p, 1 - x], rx.at[p, 0], x_send.at[p], x_recv.at[p], beside))
-    for p in range(n_parts):
-        if p % 2 == 0:
-            value = wide(ux[p, y])
-            for dy in range(1, ny):
-                remote(ux.at[p, y], ry.at[p, dy, 0], y_send.at[p, dy], y_recv.at[p, dy], ctx_at(lax.rem(y + ny - dy, ny))).wait_recv()
-                value = value + wide(ry[p, dy, 0])
-        else:
-            remote(ux.at[p, 1 - x], rx.at[p, 0], x_send.at[p], x_recv.at[p], beside).wait_recv()
-            value = wide(ux[p, x]) + wide(rx[p, 0])
+        total = x_ref[:, core, :, cols].astype(jnp.float32) + r1[p].astype(jnp.float32)
+        sb[p] = total.astype(jnp.bfloat16).reshape(nc, nz, sub, width)
+        for dc in range(1, nc):
+            ct = lax.rem(c + dc, nc)
+            launch(remote(sb.at[p, ct], r2.at[p, dc], s2_send.at[p, dc], s2_recv.at[p, dc], (ct, e)))
+
+    def stage_three(p):
+        value = sb[p, c].astype(jnp.float32)
+        for dc in range(1, nc):
+            cf = lax.rem(c + nc - dc, nc)
+            remote(sb.at[p, c], r2.at[p, dc], s2_send.at[p, dc], s2_recv.at[p, dc], (cf, e)).wait_recv()
+            value = value + r2[p, dc].astype(jnp.float32)
         tb[p] = value.astype(jnp.bfloat16)
         for dz in range(1, nz):
             zt = lax.rem(z + dz, nz)
             launch(remote(tb.at[p, zt], r3.at[p, dz], s3_send.at[p, dz], s3_recv.at[p, dz], (c, zt * 2 + core)))
-    for p in range(n_parts):
+
+    def stage_last(p):
         cols = slice(p * width, (p + 1) * width)
-        value = wide(tb[p, z])
+        value = tb[p, z].astype(jnp.float32)
         for dz in range(1, nz):
             zf = lax.rem(z + nz - dz, nz)
             remote(tb.at[p, z], r3.at[p, dz], s3_send.at[p, dz], s3_recv.at[p, dz], (c, zf * 2 + core)).wait_recv()
-            value = value + wide(r3[p, dz])
+            value = value + r3[p, dz].astype(jnp.float32)
         out_ref[:, cols] = value
+
+    ahead = min(2, n_parts)
+    for p in range(ahead):
+        stage_two(p)
+    for p in range(n_parts):
+        stage_three(p)
+        if p + ahead < n_parts:
+            stage_two(p + ahead)
+    for p in range(n_parts):
+        stage_last(p)
     for copy in sent:
         copy.wait_send()
 
@@ -380,8 +372,8 @@
 def back(moe_part, hidden):
     nc, ne = lax.axis_size("ctx"), lax.axis_size("exp")
     sub, d_model = hidden.shape
-    nz, ny = ne // 2, nc // 2
-    n_parts = 4 if d_model % 512 == 0 else 2
+    nz = ne // 2
+    n_parts = parts_of(d_model)
     width = d_model // n_parts
     vmem = pl.BlockSpec(memory_space=pltpu.VMEM)
     dma = pltpu.SemaphoreType.DMA
@@ -392,22 +384,19 @@
         in_specs=[vmem],
         out_specs=vmem,
         scratch_shapes=[
-            pltpu.VMEM((n_parts, ny, 2, nz, sub, width), bf16),
-            pltpu.VMEM((n_parts, ny, 2, nz, sub, width), bf16),
-            pltpu.VMEM((n_parts, ny, nz, sub, width), bf16),
-            pltpu.VMEM((n_parts, max(ny, 2), nz, sub, width), bf16),
-            pltpu.VMEM((n_parts, ny, 2, nz, sub, width), bf16),
+            pltpu.VMEM((n_parts, nc * nz, sub, width), bf16),
+            pltpu.VMEM((n_parts, nc, nz, sub, width), bf16),
+            pltpu.VMEM((n_parts, nc, nz, sub, width), bf16),
             pltpu.VMEM((n_parts, nz, sub, width), bf16),
             pltpu.VMEM((n_parts, nz, sub, width), bf16),
             dma((n_parts,)), dma((n_parts,)),
-            dma((n_parts,)), dma((n_parts,)),
-            dma((n_parts, ny)), dma((n_parts, ny)),
+            dma((n_parts, nc)), dma((n_parts, nc)),
             dma((n_parts, nz)), dma((n_parts, nz)),
         ],
         compiler_params=pltpu.CompilerParams(
             collective_id=1, has_side_effects=True, vmem_limit_bytes=BACK_VMEM
         ),
-    )(moe_part.reshape(ny, 2, nz, 2, sub, d_model))
+    )(moe_part.reshape(nc * nz, 2, sub, d_model))
 
 
 def fast_body(

time: 140 us -> 136 us (0.971)
  local copies, waits for them, and re-layouts: 4.94 us -> 2 us
    unnamed x12 -> x4, local copies, waits for them, and re-layouts: 3.62 us -> 0.67 us
where the time goes in v3:
time: 136 us
  Pallas kernels  103 us (76%)
  matrix products  28.8 us (21%)
  other arithmetic  2.15 us (2%)
  local copies, waits for them, and re-layouts  2 us (1%)
    pallas_call x1, Pallas kernels, front(): pl.pallas_call(functools.partial(front_kernel, nc, ne, heads), out_shape=...  67.9 us
    pallas_call x1, Pallas kernels, back(): pl.pallas_call(functools.partial(back_kernel, nc, ne), out_shape=jax.Shap...  34.7 us
    dot_general x1, matrix products, fast_body(): lax.dot_general(table, outputs.reshape(local * ne * capacity, d_model), (...  10.5 us
    dot_general x1, matrix products, fast_body(): jnp.einsum('esd,edf->esf', inputs, w_up, preferred_element_type=jnp.float32)  8.31 us
    dot_general x1, matrix products, fast_body(): jnp.dot(table, full, preferred_element_type=jnp.float32)  5.59 us
    dot_general x1, matrix products, fast_body(): jnp.einsum('esd,edf->esf', inputs, w_gate, preferred_element_type=jnp.flo...  2.99 us

profile of v3, /device:TPU:0, one launch (start us, length us, event | category | flops | bytes accessed | tf_op | source)
XLA Modules:
  0.0 135.7 jit_solution(7675332034551415829)
XLA Ops:
  0.0 0.1 compare_and_fusion.1
  0.1 1.3 reshape.134.gain_ref
  1.4 67.9 %shard_map.109 = (f32[16,3584]{1,0:T(8,128)}, bf16[4,8,16,3584]{3,2,1,0:T(8,128)(2,1)}, bf16[4,8,16,128]{3,2,1,0:T(8,128)(2,1)}) custom-call(bf16[128,1536]{1,0:T(8,128)(2,1)} %q_ref.1, bf16[128,1536]{1,0:T(8,128)(2,1)} %k_ref.1, bf16[128,1024]{1,0:T(8,128)(2,1)} %v_ref.1, bf16[1024,3584]{1,0:T(8,128)(2,1)} %w_hbm.1, bf16[16,3584]{1,0:T(8,128)(2,1)} %res_ref.1, ...), custom_call_target="tpu_custom_call" | custom-call | tf_op jit(solution)/shard_map/pallas_call | solution.py:268
  69.4 1.0 fusion.10
  70.4 0.3 fusion.2
  70.8 0.2 select_reduce_fusion
  71.0 0.2 iota_compare_fusion
  71.2 0.0 copy-start
  71.3 5.6 %convolution_convert_fusion = bf16[768,3584]{1,0:T(8,128)(2,1)S(1)} fusion(pred[768,512]{1,0:T(32,128)(4,1)S(1)} %bitcast.25, bf16[512,3584]{1,0:T(8,128)(2,1)} %bitcast.29), kind=kOutput, calls=%fused_computation.2 | convolution fusion | flops 2821324800 | bytes 9568256 | tf_op jit(solution)/shard_map/dot_general | solution.py:438
  76.9 0.7 copy-done
  77.5 3.0 %fusion.20 = f32[4,192,512]{2,1,0:T(8,128)S(1)} fusion(bf16[4,192,3584]{2,1,0:T(8,128)(2,1)S(1)} %bitcast.22, bf16[4,3584,512]{2,1,0:T(8,128)(2,1)S(1)} %copy-done), kind=kOutput, calls=%fused_computation.44 | convolution fusion | flops 2818572288 | bytes 21757952 | tf_op jit(solution)/shard_map/esd,edf->esf/dot_general | solution.py:440
  80.5 8.3 %multiply_convert_fusion.1 = bf16[4,192,512]{2,1,0:T(8,128)(2,1)S(1)} fusion(f32[4,192,512]{2,1,0:T(8,128)S(1)} %fusion.20, bf16[4,192,3584]{2,1,0:T(8,128)(2,1)S(1)} %bitcast.23, bf16[4,3584,512]{2,1,0:T(8,128)(2,1)} %param.20), kind=kOutput, calls=%fused_computation.4 | convolution fusion | flops 2820931584 | bytes 22544384 | tf_op jit(solution)/shard_map/esd,edf->esf/dot_general | solution.py:441
  88.8 0.0 copy-start.1
  88.9 10.5 %bitcast_convert_fusion = bf16[512,3584]{1,0:T(8,128)(2,1)} fusion(bf16[4,192,512]{2,1,0:T(8,128)(2,1)S(1)} %multiply_convert_fusion.1, bf16[4,512,3584]{2,1,0:T(8,128)(2,1)} %param.21, f32[4,192]{1,0:T(4,128)S(1)} %select_reduce_fusion, s32[4,512]{1,0:T(4,128)S(1)} %fusion.2), kind=kOutput, calls=%fused_computation.1 | convolution fusion | flops 5644877824 | bytes 19147776 | tf_op jit(solution)/shard_map/dot_general | solution.py:445
  99.4 34.7 %shard_map.110 = f32[16,3584]{1,0:T(8,128)} custom-call(bf16[16,2,16,3584]{3,2,1,0:T(8,128)(2,1)} %bitcast.24), custom_call_target="tpu_custom_call" | custom-call | tf_op jit(solution)/shard_map/pallas_call | solution.py:381
  134.1 0.0 copy-done.1
  134.1 1.6 %add_convert_fusion = bf16[16,3584]{1,0:T(8,128)(2,1)} fusion(f32[16,3584]{1,0:T(8,128)S(1)} %copy-done.1, f32[16,3584]{1,0:T(8,128)} %shard_map.110), kind=kLoop, calls=%fused_computation.16 | loop fusion | flops 114688 | bytes 573440 | tf_op jit(solution)/shard_map/convert_element_type | solution.py:451
  (5 shorter events, 0.0 us)
Async XLA Ops:
  71.2 6.3 %copy-start = (bf16[4,3584,512]{2,1,0:T(8,128)(2,1)S(1)}, bf16[4,3584,512]{2,1,0:T(8,128)(2,1)}, u32[]{:S(2)}) copy-start(bf16[4,3584,512]{2,1,0:T(8,128)(2,1)} %param.19) | copy-start | bytes 44040196
  88.8 45.3 %copy-start.1 = (f32[16,3584]{1,0:T(8,128)S(1)}, f32[16,3584]{1,0:T(8,128)}, u32[]{:S(2)}) copy-start(f32[16,3584]{1,0:T(8,128)} %get-tuple-element.8) | copy-start | bytes 688132
